TPU v7x, 512 devices: a whole 4x4x16 slice. The times are simulated.
512 devices in a mesh: expert: 32 (over z, core), dp: 4 (over x), tensor: 4 (over y).
Axes of the slice: x: 4, y: 4, z: 16, core: 2. Of those that a mesh axis runs over, the one named last changes fastest.
Arguments:
- tokens: bfloat16 [2, 4096, 7168], P(None, ('expert', 'dp')), may hold values from -6 to 6
- cotangent: bfloat16 [2, 4096, 7168], P(None, ('expert', 'dp')), may hold values from -0.625 to 0.625
- route_gate: bfloat16 [2, 4096, 2], P(None, ('expert', 'dp')), may hold values from 0.19921875 to 1
- routes: int32 [2, 4096, 2], P(None, ('expert', 'dp')), may hold values from 0 to 31, all different within a row; in each aligned block of 32 rows (0 to 31, 32 to 63, ..., all dimensions but the last counted through in order) at most 3 rows name the same one
- gate_weight: bfloat16 [32, 7168, 1024], P('expert', 'dp', 'tensor'), may hold values from -0.0625 to 0.0625
- up_weight: bfloat16 [32, 7168, 1024], P('expert', 'dp', 'tensor'), may hold values from -0.0625 to 0.0625
- down_weight: bfloat16 [32, 1024, 7168], P('expert', 'tensor', 'dp'), may hold values from -0.1875 to 0.1875
- dropped: int32 [32, 3], P('expert'), may hold values from 0 to 7, as said below
Outputs:
- saliency: float32 [2, 32, 1024], P(None, 'expert', 'tensor')
- compact_down: bfloat16 [32, 640, 7168], P('expert', 'tensor', 'dp')
Inputs may be any that keep to these rules, and one draw needn't show every extreme that they name: `routes`: each token names 2 different experts. Among the 32 tokens of one set on one index of expert and dp, no expert is named more than 3 times, a bound that some block reaches. `dropped`: each row lists 3 different block numbers.
All inputs are finite; a program needn't handle non-finite values.
Results may differ from a plain program's by a relative error of at most 0.001.
Values may be sent and summed in bfloat16 or wider, within the bound.
A program may use at most 128 MiB of HBM per device.

v0:
```python
import jax
import jax.numpy as jnp
from jax import lax
from jax.sharding import PartitionSpec as P

BLOCK = 128
NBLK = 8
KEEP = 5


def neuron_terms(x_recv, grad_recv, gate_recv, gate_full, up_full, down_full):
    gate_act = jnp.einsum("pscd,df->pscf", x_recv, gate_full, preferred_element_type=jnp.float32)
    up_act = jnp.einsum("pscd,df->pscf", x_recv, up_full, preferred_element_type=jnp.float32)
    hidden = jax.nn.silu(gate_act) * up_act
    product = jnp.einsum("pscd,fd->pscf", grad_recv, down_full, preferred_element_type=jnp.float32)
    hidden_grad = gate_recv.astype(jnp.float32)[..., None] * product
    return jnp.sum(hidden * hidden_grad, axis=(0, 2))


def body(tokens, cotangent, route_gate, routes, gate_weight, up_weight, down_weight, dropped):
    experts = lax.axis_size("expert")
    tensor_count = lax.axis_size("tensor")
    tensor_pos = lax.axis_index("tensor")
    tok_rows = tokens.shape[1]
    top_count = routes.shape[2]
    capacity = min(tok_rows, max(2, 3 * tok_rows * top_count // (2 * experts)))
    expert_ids = jnp.arange(experts, dtype=jnp.int32)
    matched = routes[:, :, :, None] == expert_ids
    chosen = jnp.any(matched, axis=2).astype(jnp.float32)
    weight_sum = jnp.sum(
        jnp.where(matched, route_gate.astype(jnp.float32)[:, :, :, None], 0.0), axis=2
    )
    earlier = jnp.cumsum(chosen, axis=1) - chosen
    placing = chosen[..., None] * (earlier[..., None] == jnp.arange(capacity, dtype=jnp.float32))
    slot_gate = jnp.einsum("stec,ste->esc", placing, weight_sum, precision=lax.Precision.HIGHEST)
    gate_slots = slot_gate.astype(jnp.bfloat16)
    placing_half = placing.astype(jnp.bfloat16)
    gate_rows, up_rows = (
        lax.all_gather(gate_weight, "dp", axis=1, tiled=True),
        lax.all_gather(up_weight, "dp", axis=1, tiled=True),
    )
    down_cols = lax.all_gather(down_weight, "dp", axis=2, tiled=True)
    gate_full = gate_rows[0]
    up_full = up_rows[0]
    down_full = down_cols[0]
    x_slots = jnp.einsum(
        "stec,std->escd", placing_half, tokens, preferred_element_type=jnp.float32
    ).astype(jnp.bfloat16)
    grad_slots = jnp.einsum(
        "stec,std->escd", placing_half, cotangent, preferred_element_type=jnp.float32
    ).astype(jnp.bfloat16)
    partial_terms = neuron_terms(
        lax.all_to_all(x_slots, "expert", split_axis=0, concat_axis=0, tiled=True),
        lax.all_to_all(grad_slots, "expert", split_axis=0, concat_axis=0, tiled=True),
        lax.all_to_all(gate_slots, "expert", split_axis=0, concat_axis=0, tiled=True),
        gate_full,
        up_full,
        down_full,
    )
    totals = lax.psum(partial_terms, "dp")
    saliency = jnp.abs(totals)[:, None, :]
    blocks = jnp.arange(NBLK, dtype=jnp.int32)
    kept_flag = jnp.all(dropped[0][:, None] != blocks[None, :], axis=0)
    ranking = jnp.cumsum(kept_flag.astype(jnp.int32)) - 1
    rows_out = KEEP * BLOCK // tensor_count
    whole_rows = lax.all_gather(down_weight, "tensor", axis=1, tiled=True)[0]
    target_rows = tensor_pos * rows_out + jnp.arange(rows_out, dtype=jnp.int32)
    wanted_rank = target_rows // BLOCK
    chosen_block = kept_flag[None, :] & (ranking[None, :] == wanted_rank[:, None])
    source_block = jnp.sum(jnp.where(chosen_block, blocks[None, :], 0), axis=1)
    source_rows = source_block * BLOCK + target_rows % BLOCK
    compact_down = jnp.take(whole_rows, source_rows, axis=0)[None]
    return (saliency, compact_down)


def solution(mesh):
    return jax.shard_map(
        body,
        mesh=mesh,
        in_specs=(
            P(None, ("expert", "dp"), None),
            P(None, ("expert", "dp"), None),
            P(None, ("expert", "dp"), None),
            P(None, ("expert", "dp"), None),
            P("expert", "dp", "tensor"),
            P("expert", "dp", "tensor"),
            P("expert", "tensor", "dp"),
            P("expert", None),
        ),
        out_specs=(P(None, "expert", "tensor"), P("expert", "tensor", "dp")),
        check_vma=False,
    )
```

profile of v0, /device:TPU:40, one launch (start us, length us, event | category | flops | bytes accessed | tf_op | source)
XLA Modules:
  0.0 330.8 jit_solution(15425462120463075348)
XLA Ops:
  7.2 0.8 fusion.36
  8.3 0.7 convert_element_type.58
  9.0 0.8 select_reduce_fusion
  9.8 0.6 fusion.33
  10.4 0.6 convert_element_type.59
  11.0 15.4 %all-to-all-start.1 = ((bf16[32,2,3]{2,1,0:T(2,128)(2,1)}), bf16[32,2,3]{2,1,0:T(2,128)(2,1)S(1)}, u32[]{:S(2)}, u32[]{:S(2)}) async-start(bf16[32,2,3]{2,1,0:T(2,128)(2,1)} %convert_element_type.59), calls=%async_computation.1 | async-start | bytes 32768 | tf_op jit(solution)/shard_map/all_to_all | solution.py:55
  26.5 0.7 all-gather.11.cloned.1.call-update
  27.2 0.9 fusion
  28.0 4.4 %copy.48 = bf16[32,2,3,7168]{3,1,2,0:T(2,128)(2,1)} copy(bf16[32,2,3,7168]{3,0,2,1:T(8,128)(2,1)S(1)} %fusion) | data formatting | bytes 5505024 | tf_op jit(solution)/shard_map/convert_element_type | solution.py:48
  32.4 5.1 %all-to-all-done.1 = bf16[32,2,3]{2,1,0:T(2,128)(2,1)S(1)} async-done(((bf16[32,2,3]{2,1,0:T(2,128)(2,1)}), bf16[32,2,3]{2,1,0:T(2,128)(2,1)S(1)}, u32[]{:S(2)}, u32[]{:S(2)}) %all-to-all-start.1) | async-done | bytes 416 | tf_op jit(solution)/shard_map/all_to_all | solution.py:55
  37.6 7.2 %all-to-all-start = ((bf16[32,2,3,7168]{3,1,2,0:T(2,128)(2,1)}), bf16[32,2,3,7168]{3,1,2,0:T(2,128)(2,1)}, u32[]{:S(2)}, u32[]{:S(2)}) async-start(bf16[32,2,3,7168]{3,1,2,0:T(2,128)(2,1)} %copy.48), calls=%async_computation | async-start | bytes 5505024 | tf_op jit(solution)/shard_map/all_to_all | solution.py:53
  44.9 0.7 all-gather.5.cloned.1.call-update
  45.6 0.9 fusion.1
  46.4 4.4 %copy.53 = bf16[32,2,3,7168]{3,1,2,0:T(2,128)(2,1)} copy(bf16[32,2,3,7168]{3,0,2,1:T(8,128)(2,1)S(1)} %fusion.1) | data formatting | bytes 5505024 | tf_op jit(solution)/shard_map/convert_element_type | solution.py:51
  50.8 122.4 %all-to-all-done = bf16[32,2,3,7168]{3,1,2,0:T(2,128)(2,1)} async-done(((bf16[32,2,3,7168]{3,1,2,0:T(2,128)(2,1)}), bf16[32,2,3,7168]{3,1,2,0:T(2,128)(2,1)}, u32[]{:S(2)}, u32[]{:S(2)}) %all-to-all-start) | async-done | bytes 2752544 | tf_op jit(solution)/shard_map/all_to_all | solution.py:53
  173.2 4.6 %all-to-all-start.2 = ((bf16[32,2,3,7168]{3,1,2,0:T(2,128)(2,1)}), bf16[32,2,3,7168]{3,1,2,0:T(2,128)(2,1)}, u32[]{:S(2)}, u32[]{:S(2)}) async-start(bf16[32,2,3,7168]{3,1,2,0:T(2,128)(2,1)} %copy.53), calls=%async_computation.2 | async-start | bytes 5505024 | tf_op jit(solution)/shard_map/all_to_all | solution.py:54
  177.9 0.7 all-gather.9.cloned.1.call-update
  178.6 0.2 all-gather.7.cloned.1.call-start
  178.8 0.3 all-gather.7.cloned.1.call-update
  179.1 0.1 fusion.39
  179.2 0.2 reduce-window.8
  179.4 0.1 select_reduce_fusion.1
  179.6 0.1 copy.51
  179.7 4.1 %gather_fusion = bf16[160,1792]{1,0:T(8,128)(2,1)S(1)} fusion(bf16[1024,1792]{1,0:T(8,128)(2,1)} %bitcast.57, s32[1024]{0:T(1024)S(1)} %pad_clamp_fusion), kind=kCustom, calls=%fused_computation | custom fusion | bytes 1147520 | tf_op jit(solution)/shard_map/jit(_take)/gather | solution.py:72
  183.8 0.9 bitcast_select_fusion
  184.7 3.8 %fusion.6 = f32[32,2,3,256]{3,0,2,1:T(8,128)S(1)} fusion(bf16[1,7168,256]{2,1,0:T(8,128)(2,1)} %all-gather.5.cloned.1.call-done, bf16[32,2,3,7168]{3,1,2,0:T(2,128)(2,1)} %all-to-all-done), kind=kOutput, calls=%fused_computation.9 | convolution fusion | flops 704643072 | bytes 6619136 | tf_op jit(solution)/shard_map/pscd,df->pscf/dot_general | solution.py:12
  188.5 43.6 %all-gather.9.cloned.1.call-done = bf16[1,256,7168]{2,1,0:T(8,128)(2,1)} async-done(((bf16[1,256,1792]{2,1,0:T(8,128)(2,1)}), bf16[1,256,7168]{2,1,0:T(8,128)(2,1)}) %all-gather.9.cloned.1.call-update) | async-done | bytes 3670032 | tf_op jit(solution)/shard_map/all_gather | solution.py:42
  232.1 73.0 %all-to-all-done.2 = bf16[32,2,3,7168]{3,1,2,0:T(2,128)(2,1)} async-done(((bf16[32,2,3,7168]{3,1,2,0:T(2,128)(2,1)}), bf16[32,2,3,7168]{3,1,2,0:T(2,128)(2,1)}, u32[]{:S(2)}, u32[]{:S(2)}) %all-to-all-start.2) | async-done | bytes 2752544 | tf_op jit(solution)/shard_map/all_to_all | solution.py:54
  305.1 4.3 %fusion.21 = f32[32,2,3,256]{3,0,2,1:T(8,128)S(1)} fusion(bf16[1,256,7168]{2,1,0:T(8,128)(2,1)} %all-gather.9.cloned.1.call-done, bf16[32,2,3,7168]{3,1,2,0:T(2,128)(2,1)} %all-to-all-done.2, f32[32,2,3]{0,2,1:T(4,128)S(1)} %copy.52), kind=kOutput, calls=%fused_computation.16 | convolution fusion | flops 704692224 | bytes 6619904 | tf_op jit(solution)/shard_map/pscd,fd->pscf/dot_general | solution.py:15
  309.4 3.8 %fusion.26 = f32[2,256]{1,0:T(2,128)S(1)} fusion(f32[32,2,3,256]{3,0,2,1:T(8,128)S(1)} %fusion.21, bf16[1,7168,256]{2,1,0:T(8,128)(2,1)} %all-gather.7.cloned.1.call-done, bf16[32,2,3,7168]{3,1,2,0:T(2,128)(2,1)} %all-to-all-done, f32[32,2,3,256]{3,0,2,1:T(8,128)S(1)} %fusion.6), kind=kOutput, calls=%fused_computation.17 | convolution fusion | flops 704986624 | bytes 6817792 | tf_op jit(solution)/shard_map/pscd,df->pscf/dot_general | solution.py:13
  313.2 10.5 %psum.7 = f32[2,256]{1,0:T(2,128)S(1)} all-reduce(f32[2,256]{1,0:T(2,128)S(1)} %fusion.26), channel_id=1, replica_groups=mesh['expert'=32,'dp'=4,'tensor'=4] {'dp'}, use_global_device_ids=true, to_apply=%region_4.5 | all-reduce | flops 512 | bytes 4096 | tf_op jit(solution)/shard_map/psum | solution.py:60
  323.7 0.6 broadcast_in_dim.52
  (28 shorter events, 0.6 us)
Async XLA Ops:
  7.2 20.0 %copy-start = (bf16[2,32,7168]{2,1,0:T(8,128)(2,1)S(1)}, bf16[2,32,7168]{2,1,0:T(8,128)(2,1)}, u32[]{:S(2)}) copy-start(bf16[2,32,7168]{2,1,0:T(8,128)(2,1)} %param.8) | copy-start | bytes 2752516
  11.0 26.5 %all-to-all-start.1 = ((bf16[32,2,3]{2,1,0:T(2,128)(2,1)}), bf16[32,2,3]{2,1,0:T(2,128)(2,1)S(1)}, u32[]{:S(2)}, u32[]{:S(2)}) async-start(bf16[32,2,3]{2,1,0:T(2,128)(2,1)} %convert_element_type.59), calls=%async_computation.1 | async-start | bytes 32768 | tf_op jit(solution)/shard_map/all_to_all | solution.py:55
  26.4 153.3 %all-gather.11.cloned.1.call-start = ((), (), s32[]{:S(2)}) async-start(), calls=%async_computation.6 | async-start | bytes 4587520 | tf_op jit(solution)/shard_map/all_gather | solution.py:66
  32.4 13.1 %copy-start.1 = (bf16[2,32,7168]{2,1,0:T(8,128)(2,1)S(1)}, bf16[2,32,7168]{2,1,0:T(8,128)(2,1)}, u32[]{:S(2)}) copy-start(bf16[2,32,7168]{2,1,0:T(8,128)(2,1)} %param.9) | copy-start | bytes 2752516
  37.6 135.6 %all-to-all-start = ((bf16[32,2,3,7168]{3,1,2,0:T(2,128)(2,1)}), bf16[32,2,3,7168]{3,1,2,0:T(2,128)(2,1)}, u32[]{:S(2)}, u32[]{:S(2)}) async-start(bf16[32,2,3,7168]{3,1,2,0:T(2,128)(2,1)} %copy.48), calls=%async_computation | async-start | bytes 5505024 | tf_op jit(solution)/shard_map/all_to_all | solution.py:53
  44.8 139.9 %all-gather.5.cloned.1.call-start = ((), (), s32[]{:S(2)}) async-start(), calls=%async_computation.3 | async-start | bytes 4587520 | tf_op jit(solution)/shard_map/all_gather | solution.py:39
  50.8 128.4 %copy-start.2 = (s32[1,3]{1,0:T(1,128)S(1)}, s32[1,3]{1,0:T(1,128)}, u32[]{:S(2)}) copy-start(s32[1,3]{1,0:T(1,128)} %param.15) | copy-start | bytes 40
  173.2 131.9 %all-to-all-start.2 = ((bf16[32,2,3,7168]{3,1,2,0:T(2,128)(2,1)}), bf16[32,2,3,7168]{3,1,2,0:T(2,128)(2,1)}, u32[]{:S(2)}, u32[]{:S(2)}) async-start(bf16[32,2,3,7168]{3,1,2,0:T(2,128)(2,1)} %copy.53), calls=%async_computation.2 | async-start | bytes 5505024 | tf_op jit(solution)/shard_map/all_to_all | solution.py:54
  177.8 54.3 %all-gather.9.cloned.1.call-start = ((), (), s32[]{:S(2)}) async-start(), calls=%async_computation.5 | async-start | bytes 4587520 | tf_op jit(solution)/shard_map/all_gather | solution.py:42
  178.6 130.9 %all-gather.7.cloned.1.call-start = ((), (), s32[]{:S(2)}) async-start(), calls=%async_computation.4 | async-start | bytes 4587520 | tf_op jit(solution)/shard_map/all_gather | solution.py:40
Sparse Core Ops, SparseCore 0:
  29.3 51.7 all-gather.10
  83.2 52.5 all-gather.4
  180.7 51.2 all-gather.8
  234.0 51.8 all-gather.6
where the time goes:
time: 331 us
  waiting for transfers between devices  247 us (75%)
  starting transfers between devices  27.5 us (8%)
  matrix products  14.1 us (4%)
  between operations  14 us (4%)
  local copies, waits for them, and re-layouts  13.8 us (4%)
  blocking collectives  10.5 us (3%)
  other arithmetic  4.37 us (1%)
    all_to_all x1, waiting for transfers between devices, body(): lax.all_to_all(x_slots, 'expert', split_axis=0, concat_axis=0, tiled=True)  122 us
    all_to_all x1, waiting for transfers between devices, body(): lax.all_to_all(grad_slots, 'expert', split_axis=0, concat_axis=0, tiled=T...  73 us
    all_gather x1, waiting for transfers between devices, body(): down_cols = lax.all_gather(down_weight, 'dp', axis=2, tiled=True)  43.6 us
    all_to_all x1, starting transfers between devices, body(): lax.all_to_all(gate_slots, 'expert', split_axis=0, concat_axis=0, tiled=T...  15.4 us
    psum x1, blocking collectives, body(): totals = lax.psum(partial_terms, 'dp')  10.5 us
    all_to_all x1, starting transfers between devices, body(): lax.all_to_all(x_slots, 'expert', split_axis=0, concat_axis=0, tiled=True)  7.22 us
  transfers between devices with their start and end apart: 7, of which 4 were waited for; matrix products, arithmetic and copies ran while one was open for 7% of the time, Pallas kernels for 0%

commit v1 on v0

v1 whole, which is shorter than its diff:
```python
import jax
import jax.numpy as jnp
from jax import lax
from jax.sharding import PartitionSpec as P

BLOCK = 128
NBLK = 8
KEEP = 5


def slots_of(routes, capacity, experts):
    expert_ids = jnp.arange(experts, dtype=jnp.int32)
    matched = routes[..., None] == expert_ids
    chosen = jnp.any(matched, axis=-2).astype(jnp.float32)
    earlier = jnp.cumsum(chosen, axis=-2) - chosen
    return matched, chosen[..., None] * (earlier[..., None] == jnp.arange(capacity, dtype=jnp.float32))


def compaction(down_weight, dropped, tensor_pos, tensor_count):
    blocks = jnp.arange(NBLK, dtype=jnp.int32)
    kept_flag = jnp.all(dropped[0][:, None] != blocks[None, :], axis=0)
    ranking = jnp.cumsum(kept_flag.astype(jnp.int32)) - 1
    rows_out = KEEP * BLOCK // tensor_count
    whole_rows = lax.all_gather(down_weight, "tensor", axis=1, tiled=True)[0]
    target_rows = tensor_pos * rows_out + jnp.arange(rows_out, dtype=jnp.int32)
    wanted_rank = target_rows // BLOCK
    chosen_block = kept_flag[None, :] & (ranking[None, :] == wanted_rank[:, None])
    source_block = jnp.sum(jnp.where(chosen_block, blocks[None, :], 0), axis=1)
    source_rows = source_block * BLOCK + target_rows % BLOCK
    return jnp.take(whole_rows, source_rows, axis=0)[None]


def body(tokens, cotangent, route_gate, routes, gate_weight, up_weight, down_weight, dropped):
    experts = lax.axis_size("expert")
    dp = lax.axis_size("dp")
    tensor_count = lax.axis_size("tensor")
    tensor_pos = lax.axis_index("tensor")
    rows, width = tokens.shape[1], tokens.shape[2]
    top_count = routes.shape[2]
    capacity = min(rows, max(2, 3 * rows * top_count // (2 * experts)))
    own_set = tensor_pos % 2
    mine = lax.switch(
        tensor_pos,
        [lambda: tokens[0], lambda: tokens[1], lambda: cotangent[0], lambda: cotangent[1]],
    )
    part = lax.all_to_all(mine.reshape(rows, dp, width // dp), "dp", split_axis=1, concat_axis=0, tiled=True)
    part = part.reshape(dp, rows, width // dp)
    set_routes = lax.dynamic_index_in_dim(routes, own_set, 0, keepdims=False)
    all_routes = lax.all_gather(set_routes, "dp")
    _, placing = slots_of(all_routes, capacity, experts)
    packed = jnp.einsum(
        "ptec,ptd->epcd", placing.astype(jnp.bfloat16), part, preferred_element_type=jnp.float32
    ).astype(jnp.bfloat16)
    matched, own_placing = slots_of(routes, capacity, experts)
    weight_sum = jnp.sum(jnp.where(matched, route_gate.astype(jnp.float32)[:, :, :, None], 0.0), axis=2)
    slot_gate = jnp.einsum("stec,ste->esc", own_placing, weight_sum, precision=lax.Precision.HIGHEST)
    gates = lax.all_to_all(slot_gate.astype(jnp.bfloat16), "expert", split_axis=0, concat_axis=0, tiled=True)
    arrived = lax.all_to_all(packed, "expert", split_axis=0, concat_axis=0, tiled=True)
    every = lax.all_gather(arrived, "tensor")
    x_rows, grad_rows = every[:2], every[2:]
    gate_part = jnp.einsum("sepcd,df->psecf", x_rows, gate_weight[0], preferred_element_type=jnp.float32)
    up_part = jnp.einsum("sepcd,df->psecf", x_rows, up_weight[0], preferred_element_type=jnp.float32)
    grad_part = jnp.einsum("sepcd,fd->psecf", grad_rows, down_weight[0], preferred_element_type=jnp.float32)
    sums = jnp.sum(
        lax.all_to_all(
            jnp.stack([gate_part, up_part, grad_part], axis=1), "dp", split_axis=0, concat_axis=0, tiled=True
        ),
        axis=0,
    )
    hidden = jax.nn.silu(sums[0]) * sums[1]
    hidden_grad = jnp.transpose(gates.astype(jnp.float32), (1, 0, 2))[..., None] * sums[2]
    totals = lax.psum(jnp.sum(hidden * hidden_grad, axis=(1, 2)), "dp")
    saliency = jnp.abs(totals)[:, None, :]
    return (saliency, compaction(down_weight, dropped, tensor_pos, tensor_count))


def solution(mesh):
    return jax.shard_map(
        body,
        mesh=mesh,
        in_specs=(
            P(None, ("expert", "dp"), None),
            P(None, ("expert", "dp"), None),
            P(None, ("expert", "dp"), None),
            P(None, ("expert", "dp"), None),
            P("expert", "dp", "tensor"),
            P("expert", "dp", "tensor"),
            P("expert", "tensor", "dp"),
            P("expert", None),
        ),
        out_specs=(P(None, "expert", "tensor"), P("expert", "tensor", "dp")),
        check_vma=False,
    )
```

time: 331 us -> 252 us (0.76)
  the two profiles are of different devices: /device:TPU:40 before, /device:TPU:32 now
where the time goes in v1:
time: 252 us; the launch traced here: 251 us
  blocking collectives  105 us (42%)
  waiting for transfers between devices  92.3 us (37%)
  local copies, waits for them, and re-layouts  15.8 us (6%)
  between operations  14.3 us (6%)
  starting transfers between devices  14 us (6%)
  other arithmetic  6.39 us (3%)
  matrix products  3.16 us (1%)
    all_to_all x1, blocking collectives, body(): lax.all_to_all(packed, 'expert', split_axis=0, concat_axis=0, tiled=True)  84 us
    all_gather x1, waiting for transfers between devices, body(): every = lax.all_gather(arrived, 'tensor')  49.6 us
    all_gather x1, waiting for transfers between devices, compaction(): whole_rows = lax.all_gather(down_weight, 'tensor', axis=1, tiled=True)[0]  42 us
    all_gather x1, blocking collectives, body(): all_routes = lax.all_gather(set_routes, 'dp')  10.9 us
    psum x1, blocking collectives, body(): totals = lax.psum(jnp.sum(hidden * hidden_grad, axis=(1, 2)), 'dp')  10.4 us
    all_to_all x1, starting transfers between devices, body(): lax.all_to_all(slot_gate.astype(jnp.bfloat16), 'expert', split_axis=0, co...  5.4 us
  transfers between devices with their start and end apart: 5, of which 2 were waited for; matrix products, arithmetic and copies ran while one was open for 7% of the time, Pallas kernels for 0%

profile of v1, /device:TPU:32, one launch (start us, length us, event | category | flops | bytes accessed | tf_op | source)
XLA Modules:
  0.0 251.2 jit_solution(9542712999511446499)
XLA Ops:
  7.2 1.2 conditional.1
  7.2 1.1 slice.18
  8.4 0.3 reshape.185
  8.7 0.8 copy.69
  9.5 4.3 %all-to-all-start = ((bf16[32,4,1792]{2,0,1:T(8,128)(2,1)}), bf16[32,4,1792]{2,0,1:T(8,128)(2,1)S(1)}, u32[]{:S(2)}, u32[]{:S(2)}) async-start(bf16[32,4,1792]{2,0,1:T(8,128)(2,1)} %copy.69), calls=%async_computation | async-start | bytes 917504 | tf_op jit(solution)/shard_map/all_to_all | solution.py:46
  13.8 10.9 %all_gather.13 = s32[4,32,2]{1,2,0:T(2,128)S(1)} all-gather(s32[1,32,2]{1,2,0:T(2,128)S(1)} %constant_dynamic-slice_fusion), channel_id=1, replica_groups=mesh['expert'=32,'dp'=4,'tensor'=4] {'dp'}, dimensions={0}, use_global_device_ids=true | all-gather | bytes 1280 | tf_op jit(solution)/shard_map/all_gather | solution.py:49
  24.7 0.1 fusion.24
  25.1 0.5 fusion.2
  25.6 1.1 copy.72
  26.7 84.0 %all_to_all.30 = bf16[32,4,3,1792]{3,1,2,0:T(4,128)(2,1)S(1)} all-to-all(bf16[32,4,3,1792]{3,1,2,0:T(4,128)(2,1)S(1)} %copy.72), channel_id=1, replica_groups=mesh['expert'=32,'dp'=4,'tensor'=4] {'expert'}, dimensions={0} | all-to-all | bytes 2752512 | tf_op jit(solution)/shard_map/all_to_all | solution.py:58
  110.6 1.3 copy.73
  112.0 0.7 all-gather.4.cloned.1.call-update
  113.0 1.0 multiply_reduce_fusion
  113.9 0.6 copy.110
  114.6 5.4 %all-to-all-start.3 = ((bf16[32,2,3]{2,1,0:T(2,128)(2,1)}), bf16[32,2,3]{2,1,0:T(2,128)(2,1)S(1)}, u32[]{:S(2)}, u32[]{:S(2)}) async-start(bf16[32,2,3]{2,1,0:T(2,128)(2,1)} %copy.110), calls=%async_computation.3 | async-start | bytes 32768 | tf_op jit(solution)/shard_map/all_to_all | solution.py:57
  120.1 0.2 reduce-window.8
  120.3 49.6 %all-gather.6.cloned.1.call-done = bf16[128,4,3,1792]{3,0,2,1:T(8,128)(2,1)} async-done(((bf16[32,4,3,1792]{3,0,2,1:T(8,128)(2,1)}), bf16[128,4,3,1792]{3,0,2,1:T(8,128)(2,1)}) %all-gather.6.cloned.1.call-update) | async-done | bytes 5505040 | tf_op jit(solution)/shard_map/all_gather | solution.py:59
  169.9 3.0 %fusion.35 = (bf16[64,4,3,1792]{3,0,2,1:T(8,128)(2,1)S(1)}, bf16[64,4,3,1792]{3,0,2,1:T(8,128)(2,1)S(1)}) fusion(bf16[128,4,3,1792]{3,0,2,1:T(8,128)(2,1)} %all-gather.6.cloned.1.call-done), kind=kLoop, calls=%fused_computation.67 | loop fusion | bytes 11010048 | tf_op jit(solution)/shard_map/slice | solution.py:60
  172.9 0.9 fusion.13
  173.8 0.9 fusion.10
  174.7 0.3 copy-done.4
  175.0 0.9 fusion.7
  175.9 0.3 pad_maximum_fusion
  176.2 1.6 copy.77
  177.7 4.2 %all-to-all-start.2 = ((f32[4,3,2,32,3,256]{5,3,4,2,1,0:T(8,128)}), f32[4,3,2,32,3,256]{5,3,4,2,1,0:T(8,128)S(1)}, u32[]{:S(2)}, u32[]{:S(2)}) async-start(f32[4,3,2,32,3,256]{5,3,4,2,1,0:T(8,128)} %copy.77), calls=%async_computation.2 | async-start | bytes 4718592 | tf_op jit(solution)/shard_map/all_to_all | solution.py:65
  182.3 42.0 %all-gather.4.cloned.1.call-done = bf16[1,1024,1792]{2,1,0:T(8,128)(2,1)} async-done(((bf16[1,256,1792]{2,1,0:T(8,128)(2,1)}), bf16[1,1024,1792]{2,1,0:T(8,128)(2,1)}) %all-gather.4.cloned.1.call-update) | async-done | bytes 3670032 | tf_op jit(solution)/shard_map/all_gather | solution.py:24
  224.2 4.9 %gather_fusion = bf16[160,1792]{1,0:T(8,128)(2,1)} fusion(bf16[1024,1792]{1,0:T(8,128)(2,1)} %bitcast.81, s32[1024]{0:T(1024)S(1)} %pad_clamp_fusion), kind=kCustom, calls=%fused_computation | custom fusion | bytes 1147520 | tf_op jit(solution)/shard_map/jit(_take)/gather | solution.py:30
  229.1 2.0 bitcast_select_fusion
  231.1 1.0 reduce_sum.36
  232.1 1.2 fusion.22
  233.3 10.4 %psum.7 = f32[2,256]{1,0:T(2,128)S(1)} all-reduce(f32[2,256]{1,0:T(2,128)S(1)} %fusion.22), channel_id=1, replica_groups=mesh['expert'=32,'dp'=4,'tensor'=4] {'dp'}, use_global_device_ids=true, to_apply=%region_11.12 | all-reduce | flops 512 | bytes 4096 | tf_op jit(solution)/shard_map/psum | solution.py:72
  243.8 0.6 broadcast_in_dim.35
  (41 shorter events, 1.0 us)
Async XLA Ops:
  7.2 166.6 %copy-start = (bf16[1,1792,256]{2,1,0:T(8,128)(2,1)S(1)}, bf16[1,1792,256]{2,1,0:T(8,128)(2,1)}, u32[]{:S(2)}) copy-start(bf16[1,1792,256]{2,1,0:T(8,128)(2,1)} %param.17) | copy-start | bytes 2752516
  7.2 6.6 %copy-start.2 = (s32[2,32,2]{1,2,0:T(2,128)S(1)}, s32[2,32,2]{1,2,0:T(2,128)}, u32[]{:S(2)}) copy-start(s32[2,32,2]{1,2,0:T(2,128)} %param.15) | copy-start | bytes 1540
  9.5 15.6 %all-to-all-start = ((bf16[32,4,1792]{2,0,1:T(8,128)(2,1)}), bf16[32,4,1792]{2,0,1:T(8,128)(2,1)S(1)}, u32[]{:S(2)}, u32[]{:S(2)}) async-start(bf16[32,4,1792]{2,0,1:T(8,128)(2,1)} %copy.69), calls=%async_computation | async-start | bytes 917504 | tf_op jit(solution)/shard_map/all_to_all | solution.py:46
  13.8 156.1 %all-gather.6.cloned.1.call-start = ((), (), s32[]{:S(2)}) async-start(), calls=%async_computation.5 | async-start | bytes 6881280 | tf_op jit(solution)/shard_map/all_gather | solution.py:59
  110.6 2.2 copy-start.3
  110.6 9.3 %copy-start.5 = (s32[1,3]{1,0:T(1,128)S(1)}, s32[1,3]{1,0:T(1,128)}, u32[]{:S(2)}) copy-start(s32[1,3]{1,0:T(1,128)} %param.19) | copy-start | bytes 40
  111.9 112.3 %all-gather.4.cloned.1.call-start = ((), (), s32[]{:S(2)}) async-start(), calls=%async_computation.4 | async-start | bytes 4587520 | tf_op jit(solution)/shard_map/all_gather | solution.py:24
  114.6 63.2 %all-to-all-start.3 = ((bf16[32,2,3]{2,1,0:T(2,128)(2,1)}), bf16[32,2,3]{2,1,0:T(2,128)(2,1)S(1)}, u32[]{:S(2)}, u32[]{:S(2)}) async-start(bf16[32,2,3]{2,1,0:T(2,128)(2,1)} %copy.110), calls=%async_computation.3 | async-start | bytes 32768 | tf_op jit(solution)/shard_map/all_to_all | solution.py:57
  120.3 52.6 %copy-start.1 = (bf16[1,256,1792]{2,1,0:T(8,128)(2,1)S(1)}, bf16[1,256,1792]{2,1,0:T(8,128)(2,1)}, u32[]{:S(2)}) copy-start(bf16[1,256,1792]{2,1,0:T(8,128)(2,1)} %param.18) | copy-start | bytes 2752516
  173.8 1.2 copy-start.4
  177.7 53.3 %all-to-all-start.2 = ((f32[4,3,2,32,3,256]{5,3,4,2,1,0:T(8,128)}), f32[4,3,2,32,3,256]{5,3,4,2,1,0:T(8,128)S(1)}, u32[]{:S(2)}, u32[]{:S(2)}) async-start(f32[4,3,2,32,3,256]{5,3,4,2,1,0:T(8,128)} %copy.77), calls=%async_computation.2 | async-start | bytes 4718592 | tf_op jit(solution)/shard_map/all_to_all | solution.py:65
Sparse Core Ops, SparseCore 0:
  112.0 57.7 all-gather.5
  172.0 52.2 all-gather.3

commit v2 on v1

v2 whole, which is shorter than its diff:
```python
import functools

import jax
import jax.numpy as jnp
from jax import lax
from jax.experimental import pallas as pl
from jax.experimental.pallas import tpu as pltpu
from jax.sharding import PartitionSpec as P

BLOCK = 128
NBLK = 8
KEEP = 5
CAP = 3
MESH = pl.DeviceIdType.MESH


def kernel(
    experts,
    tokens, cotangent, info, gate_w, up_w, down_w,
    out,
    mine, raw, info_own, info_all, packed, gate_send, gate_recv, arrived, wg, wu, wd, partial, sums, products, share, shares,
    local_sem, raw_send, raw_recv, info_send, info_recv, z_send, z_recv, g_send, g_recv,
    y_send, y_recv, f_send, f_recv, r_send, r_recv, s_send, s_recv,
):
    planes = experts // 2
    steps = planes // 2
    rows = tokens.shape[1]
    width = tokens.shape[2]
    lanes = width // 8
    slab = 8 * CAP // 8
    e = lax.axis_index("expert")
    p = lax.axis_index("dp")
    t = lax.axis_index("tensor")
    z = e // 2
    c = e % 2
    b = 2 * p + c

    def local(src, dst, sem):
        return pltpu.make_async_copy(src, dst, sem)

    def remote(src, dst, send, recv, expert, dp, tensor):
        return pltpu.make_async_remote_copy(
            src_ref=src, dst_ref=dst, send_sem=send, recv_sem=recv,
            device_id={"expert": expert, "dp": dp, "tensor": tensor}, device_id_type=MESH,
        )

    for index in range(4):
        source = tokens if index < 2 else cotangent

        @pl.when(t == index)
        def _():
            local(source.at[index % 2], mine, local_sem.at[0]).start()

    copies = [local(gate_w.at[0], wg, local_sem.at[1]), local(up_w.at[0], wu, local_sem.at[2]),
              local(down_w.at[0], wd, local_sem.at[3])]
    for copy in copies:
        copy.start()

    barrier = pltpu.get_barrier_semaphore()

    def greet(expert, dp, tensor):
        pl.semaphore_signal(
            barrier, inc=1, device_id={"expert": expert, "dp": dp, "tensor": tensor}, device_id_type=MESH
        )

    def greet_z(k, carry):
        greet((e + k) % experts, p, t)
        return carry

    lax.fori_loop(1, experts, greet_z, 0)
    for k in range(1, 4):
        greet(e, (p + k) % 4, t)
        greet(2 * z + 1 - c, (p + k) % 4, t)
        greet(e, p, (t + k) % 4)

    lane = lax.broadcasted_iota(jnp.int32, (2, 8, 128), 2)
    own_lanes = lane // rows == b % 4
    info_own[...] = jnp.where(own_lanes, info[...], 0.0)
    info_all[b] = info_own[...]
    local(tokens.at[0], mine, local_sem.at[0]).wait()
    pl.semaphore_wait(barrier, experts - 1 + 9)

    def raw_copy(k, other, owner):
        return remote(
            mine.at[:, pl.ds(pl.multiple_of(other * lanes, 128), lanes)], raw.at[owner],
            raw_send.at[k], raw_recv.at[k], 2 * z + other % 2, other // 2, t,
        )

    def info_copy(k, other, owner):
        return remote(
            info_own, info_all.at[owner], info_send.at[k], info_recv.at[k], 2 * z + other % 2, other // 2, t
        )

    own_raw = local(mine.at[:, pl.ds(pl.multiple_of(b * lanes, 128), lanes)], raw.at[b], local_sem.at[4])
    own_raw.start()
    for k in range(1, 8):
        info_copy(k, (b + k) % 8, b).start()
    for k in range(1, 8):
        raw_copy(k, (b + k) % 8, b).start()
    for k in range(1, 8):
        info_copy(k, (b + k) % 8, (b + 8 - k) % 8).wait_recv()

    count = 8 * rows

    def places(which):
        low = info_all[0, which] + info_all[1, which] + info_all[2, which] + info_all[3, which]
        high = info_all[4, which] + info_all[5, which] + info_all[6, which] + info_all[7, which]
        both = jnp.concatenate([low, high], axis=1)
        expert_of = lax.broadcasted_iota(jnp.int32, (experts, count), 0).astype(jnp.float32)
        first = jnp.broadcast_to(both[0:1], (experts, count)) == expert_of
        second = jnp.broadcast_to(both[1:2], (experts, count)) == expert_of
        chosen = jnp.where(first | second, 1.0, 0.0)
        above = lax.broadcasted_iota(jnp.int32, (count, count), 0)
        across = lax.broadcasted_iota(jnp.int32, (count, count), 1)
        before = jnp.where((above < across) & (above // rows == across // rows), 1.0, 0.0)
        rank = jnp.dot(
            chosen.astype(jnp.bfloat16), before.astype(jnp.bfloat16), preferred_element_type=jnp.float32
        )
        block_of = lax.broadcasted_iota(jnp.int32, (experts, count), 1) // rows
        place = jnp.where(chosen > 0.0, rank + CAP * block_of.astype(jnp.float32), -1.0)
        weight = jnp.where(first, jnp.broadcast_to(both[2:3], (experts, count)), 0.0) + jnp.where(
            second, jnp.broadcast_to(both[3:4], (experts, count)), 0.0
        )
        return place, weight

    group = 8
    slot_of = lax.broadcasted_iota(jnp.int32, (group, 8 * CAP, count), 1).astype(jnp.float32)

    def chosen_rows(place, start):
        part = place[start:start + group]
        return jnp.where(jnp.broadcast_to(part[:, None, :], slot_of.shape) == slot_of, 1.0, 0.0)

    place, _ = places(t % 2)
    for k in range(1, 8):
        raw_copy(k, (b + k) % 8, (b + 8 - k) % 8).wait_recv()
    own_raw.wait()
    whole = raw[...].reshape(count, lanes)
    for start in range(0, experts, group):
        select = chosen_rows(place, start).reshape(group * 8 * CAP, count).astype(jnp.bfloat16)
        values = jnp.dot(select, whole, preferred_element_type=jnp.float32)
        packed[slab * start:slab * (start + group)] = values.reshape(slab * group, 8, lanes).astype(jnp.bfloat16)

    def plane(i, sign):
        return (z + (i + 1 if sign else planes - (i + 1) % steps)) % planes

    def z_copy(i, sign, core, owner_core):
        expert = 2 * plane(i, sign) + core
        return remote(
            packed.at[pl.ds(expert * slab, slab)], arrived.at[i, t, sign, owner_core],
            z_send.at[i, sign, core], z_recv.at[i, sign, owner_core], expert, p, t,
        )

    def z_start(i, carry):
        for sign in range(2):
            for core in range(2):
                if sign == 1:
                    z_copy(i, 1, core, c).start()
                else:
                    @pl.when((i != steps - 1) | (c != core))
                    def _():
                        z_copy(i, 0, core, c).start()
        return carry

    own_slab = local(packed.at[pl.ds(e * slab, slab)], arrived.at[steps - 1, t, 0, c], z_recv.at[steps - 1, 0, c])
    own_slab.start()
    lax.fori_loop(0, steps, z_start, 0)

    gate_place, gate_weight = places(p % 2)
    row_at = lax.broadcasted_iota(jnp.int32, (group, 8 * CAP, 128), 1)
    lane_at = lax.broadcasted_iota(jnp.int32, (group, 8 * CAP, 128), 2)
    ones = jnp.ones((count, 128), jnp.bfloat16)
    for start in range(0, experts, group):
        part = gate_weight[start:start + group]
        weighted = chosen_rows(gate_place, start) * jnp.broadcast_to(part[:, None, :], slot_of.shape)
        spread = jnp.dot(
            weighted.reshape(group * 8 * CAP, count).astype(jnp.bfloat16), ones, preferred_element_type=jnp.float32
        ).reshape(group, 8 * CAP, 128)
        line = jnp.sum(jnp.where(row_at == lane_at, spread, 0.0), axis=1, keepdims=True)
        gate_send[start:start + group] = jnp.broadcast_to(line, (group, 8, 128))

    def g_copy(i, sign, core):
        expert = 2 * plane(i, sign) + core
        return remote(
            gate_send.at[expert], gate_recv.at[i], g_send.at[i, core], g_recv.at[i], expert, p, t
        )

    own_gate = local(gate_send.at[e], gate_recv.at[steps - 1], g_recv.at[steps - 1])

    def g_each(act):
        def g_step(i, carry):
            for core in range(2):
                @pl.when((c == 0) & (p // 2 == 1))
                def _():
                    act(g_copy(i, 1, core))

                @pl.when((c == 0) & (p // 2 == 0) & ((i != steps - 1) | (c != core)))
                def _():
                    act(g_copy(i, 0, core))
            return carry

        lax.fori_loop(0, steps, g_step, 0)

    g_each(lambda copy: copy.start())

    @pl.when((c == 0) & (p // 2 == 0))
    def _():
        own_gate.start()

    up_t, down_t, far_t = (t + 1) % 4, (t + 3) % 4, (t + 2) % 4

    def y_copy(i, way, owner):
        return remote(
            arrived.at[i, owner], arrived.at[i, owner], y_send.at[i, way], y_recv.at[i, way],
            e, p, up_t if way == 0 else down_t,
        )

    def f_copy(i, way, owner):
        return remote(
            arrived.at[i, owner, way], arrived.at[i, owner, way], f_send.at[i, way], f_recv.at[i, way],
            e, p, up_t if way == 0 else down_t,
        )

    def r_copy(i, k, owner):
        other = (p + k) % 4
        return remote(
            partial.at[i, other], sums.at[i, owner], r_send.at[i, k - 1], r_recv.at[i, k - 1], e, other, t
        )

    def take_z(i):
        for sign in range(2):
            for core in range(2):
                z_copy(i, sign, core, core).wait_recv()
        y_copy(i, 0, t).start()
        y_copy(i, 1, t).start()

    def take_y(i):
        y_copy(i, 0, down_t).wait_recv()
        f_copy(i, 0, down_t).start()
        y_copy(i, 1, up_t).wait_recv()
        f_copy(i, 1, up_t).start()

    def lhs(i, first, core):
        loaded = arrived[i, first:first + 2, :, core]
        return loaded.astype(jnp.float32).reshape(4 * 8 * CAP, lanes).astype(jnp.bfloat16)

    def multiply(i):
        f_copy(i, 0, far_t).wait_recv()
        f_copy(i, 1, far_t).wait_recv()
        low, high = lhs(i, 0, 0), lhs(i, 0, 1)
        grad_low, grad_high = lhs(i, 2, 0), lhs(i, 2, 1)

        def plain(weight):
            return jnp.dot(low, weight[:lanes], preferred_element_type=jnp.float32) + jnp.dot(
                high, weight[lanes:], preferred_element_type=jnp.float32
            )

        turned = (((1,), (1,)), ((), ()))
        results = (
            plain(wg),
            plain(wu),
            lax.dot_general(grad_low, wd[:, :lanes], turned, preferred_element_type=jnp.float32)
            + lax.dot_general(grad_high, wd[:, lanes:], turned, preferred_element_type=jnp.float32),
        )
        for index, value in enumerate(results):
            for which in range(2):
                for sign in range(2):
                    at = (2 * which + sign) * 8 * CAP
                    partial[i, 2 * sign + which, index] = value[at:at + 8 * CAP]
        for k in range(1, 4):
            r_copy(i, k, p).start()

    def finish(i):
        total = partial[i, p]
        for k in range(1, 4):
            r_copy(i, k, (p + 4 - k) % 4).wait_recv()
            total = total + sums[i, (p + 4 - k) % 4]
        hidden = total[0] / (1.0 + jnp.exp(-total[0])) * total[1]
        products[i] = hidden * total[2]

    for copy in copies:
        copy.wait()

    def step(s, carry):
        @pl.when((s >= 1) & (s < steps + 1))
        def _():
            take_y(s - 1)

        @pl.when(s < steps)
        def _():
            take_z(s)

        @pl.when((s >= 1) & (s < steps + 1))
        def _():
            multiply(s - 1)

        @pl.when(s >= 2)
        def _():
            finish(s - 2)
        return carry

    lax.fori_loop(0, steps + 2, step, 0)

    row24 = lax.broadcasted_iota(jnp.int32, (8 * CAP, 128), 0)
    lane24 = lax.broadcasted_iota(jnp.int32, (8 * CAP, 128), 1)

    def weigh(i, total):
        local(gate_send.at[e], gate_recv.at[i], g_recv.at[i]).wait()
        line = gate_recv[i]
        column = jnp.sum(
            jnp.where(row24 == lane24, jnp.broadcast_to(line[0:1], (8 * CAP, 128)), 0.0), axis=1, keepdims=True
        )
        return total + column * products[i]

    total = lax.fori_loop(0, steps, weigh, jnp.zeros((8 * CAP, products.shape[2]), jnp.float32))
    share[...] = jnp.broadcast_to(jnp.sum(total, axis=0, keepdims=True), share.shape)
    shares[p] = share[...]

    def s_copy(k, owner):
        return remote(share, shares.at[owner], s_send.at[k - 1], s_recv.at[k - 1], e, (p + k) % 4, t)

    for k in range(1, 4):
        s_copy(k, p).start()
    for k in range(1, 4):
        s_copy(k, (p + 4 - k) % 4).wait_recv()
    out[0] = jnp.abs(shares[0] + shares[2])
    out[1] = jnp.abs(shares[1] + shares[3])

    for k in range(1, 4):
        s_copy(k, p).wait_send()
    for k in range(1, 8):
        info_copy(k, (b + k) % 8, b).wait_send()
        raw_copy(k, (b + k) % 8, b).wait_send()
    g_each(lambda copy: copy.wait_send())

    def drain(i, carry):
        for sign in range(2):
            for core in range(2):
                if sign == 1:
                    z_copy(i, 1, core, c).wait_send()
                else:
                    @pl.when((i != steps - 1) | (c != core))
                    def _():
                        z_copy(i, 0, core, c).wait_send()
        for way in range(2):
            y_copy(i, way, t).wait_send()
            f_copy(i, way, down_t if way == 0 else up_t).wait_send()
        for k in range(1, 4):
            r_copy(i, k, p).wait_send()
        return carry

    lax.fori_loop(0, steps, drain, 0)


def routed(tokens, cotangent, info, gate_weight, up_weight, down_weight, experts):
    steps = experts // 4
    rows, width = tokens.shape[1:]
    lanes = width // 8
    depth, columns = gate_weight.shape[1:]
    slab = CAP
    anywhere = pl.BlockSpec(memory_space=pl.ANY)
    vmem = pl.BlockSpec(memory_space=pltpu.VMEM)
    half, full, dma = jnp.bfloat16, jnp.float32, pltpu.SemaphoreType.DMA
    return pl.pallas_call(
        functools.partial(kernel, experts),
        out_shape=jax.ShapeDtypeStruct((2, 8, columns), full),
        in_specs=[anywhere, anywhere, vmem, anywhere, anywhere, anywhere],
        out_specs=vmem,
        scratch_shapes=[
            pltpu.VMEM((rows, width), half),
            pltpu.VMEM((8, rows, lanes), half),
            pltpu.VMEM((2, 8, 128), full),
            pltpu.VMEM((8, 2, 8, 128), full),
            pltpu.VMEM((experts * slab, 8, lanes), half),
            pltpu.VMEM((experts, 8, 128), full),
            pltpu.VMEM((steps, 8, 128), full),
            pltpu.VMEM((steps, 4, 2, 2, slab, 8, lanes), half),
            pltpu.VMEM((depth, columns), half),
            pltpu.VMEM((depth, columns), half),
            pltpu.VMEM((columns, depth), half),
            pltpu.VMEM((steps, 4, 3, 8 * CAP, columns), full),
            pltpu.VMEM((steps, 4, 3, 8 * CAP, columns), full),
            pltpu.VMEM((steps, 8 * CAP, columns), full),
            pltpu.VMEM((8, columns), full),
            pltpu.VMEM((4, 8, columns), full),
            dma((5,)),
            dma((8,)), dma((8,)), dma((8,)), dma((8,)),
            dma((steps, 2, 2)), dma((steps, 2, 2)),
            dma((steps, 2)), dma((steps,)),
            dma((steps, 2)), dma((steps, 2)), dma((steps, 2)), dma((steps, 2)),
            dma((steps, 3)), dma((steps, 3)), dma((3,)), dma((3,)),
        ],
        compiler_params=pltpu.CompilerParams(
            collective_id=0, has_side_effects=True, vmem_limit_bytes=40 * 1024 * 1024
        ),
        cost_estimate=pl.CostEstimate(flops=4 * 10**9, transcendentals=10**5, bytes_accessed=2 * 10**8),
    )(tokens, cotangent, info, gate_weight, up_weight, down_weight)


def compaction(down_weight, dropped, tensor_pos, tensor_count):
    blocks = jnp.arange(NBLK, dtype=jnp.int32)
    kept_flag = jnp.all(dropped[0][:, None] != blocks[None, :], axis=0)
    ranking = jnp.cumsum(kept_flag.astype(jnp.int32)) - 1
    rows_out = KEEP * BLOCK // tensor_count
    whole_rows = lax.all_gather(down_weight, "tensor", axis=1, tiled=True)[0]
    target_rows = tensor_pos * rows_out + jnp.arange(rows_out, dtype=jnp.int32)
    wanted_rank = target_rows // BLOCK
    chosen_block = kept_flag[None, :] & (ranking[None, :] == wanted_rank[:, None])
    source_block = jnp.sum(jnp.where(chosen_block, blocks[None, :], 0), axis=1)
    source_rows = source_block * BLOCK + target_rows % BLOCK
    return jnp.take(whole_rows, source_rows, axis=0)[None]


def body(tokens, cotangent, route_gate, routes, gate_weight, up_weight, down_weight, dropped):
    experts = lax.axis_size("expert")
    tensor_count = lax.axis_size("tensor")
    tensor_pos = lax.axis_index("tensor")
    lines = jnp.concatenate([routes.astype(jnp.float32), route_gate.astype(jnp.float32)], axis=2)
    lines = jnp.transpose(lines, (0, 2, 1))
    info = jnp.pad(jnp.tile(lines, (1, 1, 4)), ((0, 0), (0, 4), (0, 0)))
    values = routed(tokens, cotangent, info, gate_weight, up_weight, down_weight, experts)
    saliency = values[:, :1]
    return (saliency, compaction(down_weight, dropped, tensor_pos, tensor_count))


def solution(mesh):
    return jax.shard_map(
        body,
        mesh=mesh,
        in_specs=(
            P(None, ("expert", "dp"), None),
            P(None, ("expert", "dp"), None),
            P(None, ("expert", "dp"), None),
            P(None, ("expert", "dp"), None),
            P("expert", "dp", "tensor"),
            P("expert", "dp", "tensor"),
            P("expert", "tensor", "dp"),
            P("expert", None),
        ),
        out_specs=(P(None, "expert", "tensor"), P("expert", "tensor", "dp")),
        check_vma=False,
    )
```

time: 252 us -> 145 us (0.58)
  the two profiles are of different devices: /device:TPU:32 before, /device:TPU:8 now
where the time goes in v2:
time: 145 us; the launch traced here: 144 us
  Pallas kernels  116 us (80%)
  between operations  14.1 us (10%)
  local copies, waits for them, and re-layouts  10.6 us (7%)
  other arithmetic  2.73 us (2%)
    pallas_call x1, Pallas kernels, routed(): pl.pallas_call(functools.partial(kernel, experts), out_shape=jax.ShapeDty...  116 us
    unnamed x12, local copies, waits for them, and re-layouts  5.9 us
    gather x1, local copies, waits for them, and re-layouts, compaction(): return jnp.take(whole_rows, source_rows, axis=0)[None]  4.06 us
  transfers between devices with their start and end apart: 1, of which 0 were waited for; matrix products, arithmetic and copies ran while one was open for 2% of the time, Pallas kernels for 80%

profile of v2, /device:TPU:8, one launch (start us, length us, event | category | flops | bytes accessed | tf_op | source)
XLA Modules:
  0.0 144.4 jit_solution(7429736849897757474)
XLA Ops:
  7.2 0.0 all-gather.2.cloned.1.call-start
  7.2 0.7 all-gather.2.cloned.1.call-update
  7.9 0.7 convert_element_type.23
  8.6 0.7 convert_element_type.24
  9.3 0.1 tile.10
  9.4 0.0 copy-start
  9.4 1.2 copy-done
  10.6 0.0 copy-start.1
  10.6 1.2 copy-done.1
  11.7 0.0 copy-start.2
  11.7 1.2 copy-done.2
  12.9 0.0 copy-start.3
  12.9 1.2 copy-done.3
  14.1 0.0 copy-start.4
  14.1 1.2 copy-done.4
  15.3 0.0 copy-start.5
  15.3 116.2 %shard_map.95 = f32[2,8,256]{2,1,0:T(8,128)S(1)} custom-call(bf16[2,32,7168]{2,1,0:T(8,128)(2,1)S(1)} %copy-done.1, bf16[2,32,7168]{2,1,0:T(8,128)(2,1)S(1)} %copy-done.2, f32[2,8,128]{2,1,0:T(8,128)S(1)} %pad.4.info, bf16[1,1792,256]{2,1,0:T(8,128)(2,1)S(1)} %copy-done.3, bf16[1,1792,256]{2,1,0:T(8,128)(2,1)S(1)} %copy-done.4, bf16[1,256,1792]{2,1,0:T(8,128)(2,1)S(1)} %copy-done), custom_call_target="tpu_custom_call" | custom-call | flops 4000000000 | bytes 200000000 | tf_op jit(solution)/shard_map/pallas_call | solution.py:363
  131.5 0.6 slice.3
  132.0 0.0 copy-done.5
  132.0 0.1 fusion
  132.1 0.2 reduce-window.8
  132.3 0.1 select_reduce_fusion
  132.5 0.0 all-gather.2.cloned.1.call-done
  132.5 4.1 %gather_fusion = bf16[160,1792]{1,0:T(8,128)(2,1)S(1)} fusion(bf16[1024,1792]{1,0:T(8,128)(2,1)} %bitcast.12, s32[1024]{0:T(1024)S(1)} %pad_clamp_fusion), kind=kCustom, calls=%fused_computation | custom fusion | bytes 1147520 | tf_op jit(solution)/shard_map/jit(_take)/gather | solution.py:410
  136.6 0.9 bitcast_select_fusion
  (10 shorter events, 0.1 us)
Async XLA Ops:
  7.2 125.3 %all-gather.2.cloned.1.call-start = ((), (), s32[]{:S(2)}) async-start(), calls=%async_computation | async-start | bytes 4587520 | tf_op jit(solution)/shard_map/all_gather | solution.py:404
  9.4 1.2 copy-start
  10.6 1.2 copy-start.1
  11.7 1.2 copy-start.2
  12.9 1.2 copy-start.3
  14.1 1.2 copy-start.4
  15.3 116.8 %copy-start.5 = (s32[1,3]{1,0:T(1,128)S(1)}, s32[1,3]{1,0:T(1,128)}, u32[]{:S(2)}) copy-start(s32[1,3]{1,0:T(1,128)} %param.15) | copy-start | bytes 40
Sparse Core Ops, SparseCore 0:
  10.1 68.6 all-gather.1

commit v3 on v2

--- a/solution.py
+++ b/solution.py
@@ -8,19 +8,22 @@
 from jax.sharding import PartitionSpec as P
 
 BLOCK = 128
-NBLK = 8
 KEEP = 5
 CAP = 3
 MESH = pl.DeviceIdType.MESH
+UNIT = 32
+WINDOW = 3
+OFFERS = ((0, 1, 5, 3), (1, 0, 0, 5), (1, 2, 10, 5), (1, 3, 15, 1), (2, 0, 4, 1), (2, 1, 5, 5), (2, 3, 15, 5), (3, 2, 12, 3))
+HOLDERS = ((0, 1), (0, 1, 2), (1, 2), (1, 2, 3), (2, 3))
 
 
 def kernel(
     experts,
-    tokens, cotangent, info, gate_w, up_w, down_w,
-    out,
-    mine, raw, info_own, info_all, packed, gate_send, gate_recv, arrived, wg, wu, wd, partial, sums, products, share, shares,
+    tokens, cotangent, routes, route_gate, dropped, gate_w, up_w, down_w,
+    out, compact,
+    mine, own_routes, own_gates, raw, info_own, info_all, packed, gate_send, gate_recv, arrived, wg, wu, wd, partial, sums, acc, share, shares, offered, taken,
     local_sem, raw_send, raw_recv, info_send, info_recv, z_send, z_recv, g_send, g_recv,
-    y_send, y_recv, f_send, f_recv, r_send, r_recv, s_send, s_recv,
+    y_send, y_recv, f_send, f_recv, r_send, r_recv, s_send, s_recv, c_send, c_recv,
 ):
     planes = experts // 2
     steps = planes // 2
@@ -53,6 +56,9 @@
 
     copies = [local(gate_w.at[0], wg, local_sem.at[1]), local(up_w.at[0], wu, local_sem.at[2]),
               local(down_w.at[0], wd, local_sem.at[3])]
+    small = [local(routes, own_routes, local_sem.at[5]), local(route_gate, own_gates, local_sem.at[6])]
+    for copy in small:
+        copy.start()
     for copy in copies:
         copy.start()
 
@@ -73,10 +79,31 @@
         greet(2 * z + 1 - c, (p + k) % 4, t)
         greet(e, p, (t + k) % 4)
 
-    lane = lax.broadcasted_iota(jnp.int32, (2, 8, 128), 2)
+    for copy in small:
+        copy.wait()
+    lane = lax.broadcasted_iota(jnp.int32, (2, 128), 1)
     own_lanes = lane // rows == b % 4
-    info_own[...] = jnp.where(own_lanes, info[...], 0.0)
+    spread_of = jnp.where(
+        lax.broadcasted_iota(jnp.int32, (rows, 128), 0) == lax.broadcasted_iota(jnp.int32, (rows, 128), 1) % rows, 1.0, 0.0
+    ).astype(jnp.bfloat16)
+    info_own[...] = jnp.zeros(info_own.shape, jnp.float32)
+    for which in range(2):
+        for at, lines in ((0, own_routes[which].astype(jnp.float32)), (2, own_gates[which].astype(jnp.float32))):
+            wide = jnp.dot(lines.astype(jnp.bfloat16), spread_of, preferred_element_type=jnp.float32)
+            info_own[which, at:at + 2] = jnp.where(own_lanes, wide, 0.0)
     info_all[b] = info_own[...]
+    first, second, third = dropped[0, 0], dropped[0, 1], dropped[0, 2]
+    least = jnp.minimum(first, jnp.minimum(second, third))
+    most = jnp.maximum(first, jnp.maximum(second, third))
+    middle = first + second + third - least - most
+    kept = []
+    for rank in range(KEEP):
+        number = jnp.where(least <= rank, rank + 1, rank)
+        number = jnp.where(middle <= number, number + 1, number)
+        kept.append(jnp.where(most <= number, number + 1, number))
+    copies[2].wait()
+    for rank in range(KEEP):
+        offered[rank * BLOCK:(rank + 1) * BLOCK] = jnp.where(kept[rank] == 2 * t, wd[:BLOCK], wd[BLOCK:])
     local(tokens.at[0], mine, local_sem.at[0]).wait()
     pl.semaphore_wait(barrier, experts - 1 + 9)
 
@@ -97,6 +124,21 @@
         info_copy(k, (b + k) % 8, b).start()
     for k in range(1, 8):
         raw_copy(k, (b + k) % 8, b).start()
+
+    def offer(holder, taker, start, size):
+        away = (taker - holder) % 4 - 1
+        return remote(
+            offered.at[pl.ds(start * UNIT, size * UNIT)], taken.at[away, pl.ds((start - KEEP * taker) * UNIT, size * UNIT)],
+            c_send.at[away], c_recv.at[away], e, p, taker,
+        )
+
+    def each_offer(act):
+        for entry in OFFERS:
+            @pl.when(t == entry[0])
+            def _():
+                act(offer(*entry))
+
+    each_offer(lambda copy: copy.start())
     for k in range(1, 8):
         info_copy(k, (b + k) % 8, (b + 8 - k) % 8).wait_recv()
 
@@ -156,14 +198,28 @@
                 if sign == 1:
                     z_copy(i, 1, core, c).start()
                 else:
-                    @pl.when((i != steps - 1) | (c != core))
+                    @pl.when(i != steps - 1)
                     def _():
                         z_copy(i, 0, core, c).start()
         return carry
 
+    def z_sent(i):
+        for sign in range(2):
+            for core in range(2):
+                if sign == 1:
+                    z_copy(i, 1, core, c).wait_send()
+                else:
+                    @pl.when((i != steps - 1) | (c != core))
+                    def _():
+                        z_copy(i, 0, core, c).wait_send()
+
     own_slab = local(packed.at[pl.ds(e * slab, slab)], arrived.at[steps - 1, t, 0, c], z_recv.at[steps - 1, 0, c])
     own_slab.start()
-    lax.fori_loop(0, steps, z_start, 0)
+    for core in range(2):
+        @pl.when(c != core)
+        def _():
+            z_copy(steps - 1, 0, core, c).start()
+    lax.fori_loop(0, min(WINDOW, steps), z_start, 0)
 
     gate_place, gate_weight = places(p % 2)
     row_at = lax.broadcasted_iota(jnp.int32, (group, 8 * CAP, 128), 1)
@@ -176,7 +232,7 @@
             weighted.reshape(group * 8 * CAP, count).astype(jnp.bfloat16), ones, preferred_element_type=jnp.float32
         ).reshape(group, 8 * CAP, 128)
         line = jnp.sum(jnp.where(row_at == lane_at, spread, 0.0), axis=1, keepdims=True)
-        gate_send[start:start + group] = jnp.broadcast_to(line, (group, 8, 128))
+        gate_send[start:start + group] = line
 
     def g_copy(i, sign, core):
         expert = 2 * plane(i, sign) + core
@@ -208,9 +264,9 @@
 
     up_t, down_t, far_t = (t + 1) % 4, (t + 3) % 4, (t + 2) % 4
 
-    def y_copy(i, way, owner):
-        return remote(
-            arrived.at[i, owner], arrived.at[i, owner], y_send.at[i, way], y_recv.at[i, way],
+    def y_copy(i, sign, way, owner):
+        return remote(
+            arrived.at[i, owner, sign], arrived.at[i, owner, sign], y_send.at[i, sign, way], y_recv.at[i, sign, way],
             e, p, up_t if way == 0 else down_t,
         )
 
@@ -226,18 +282,34 @@
             partial.at[i, other], sums.at[i, owner], r_send.at[i, k - 1], r_recv.at[i, k - 1], e, other, t
         )
 
-    def take_z(i):
-        for sign in range(2):
-            for core in range(2):
-                z_copy(i, sign, core, core).wait_recv()
-        y_copy(i, 0, t).start()
-        y_copy(i, 1, t).start()
-
-    def take_y(i):
-        y_copy(i, 0, down_t).wait_recv()
-        f_copy(i, 0, down_t).start()
-        y_copy(i, 1, up_t).wait_recv()
-        f_copy(i, 1, up_t).start()
+    def take_z(i, sign):
+        for core in range(2):
+            z_copy(i, sign, core, core).wait_recv()
+        y_copy(i, sign, 0, t).start()
+        y_copy(i, sign, 1, t).start()
+
+    def take_y(i, sign):
+        owner = down_t if sign == 0 else up_t
+        y_copy(i, sign, sign, owner).wait_recv()
+        f_copy(i, sign, owner).start()
+
+    def take_compact():
+        for entry in OFFERS:
+            @pl.when(t == entry[1])
+            def _():
+                offer(*entry).wait_recv()
+        for taker in range(4):
+            @pl.when(t == taker)
+            def _():
+                for unit in range(KEEP):
+                    rank = (KEEP * taker + unit) // 4
+                    at = (KEEP * taker + unit) * UNIT
+                    value = offered[at:at + UNIT]
+                    for holder in HOLDERS[rank]:
+                        if holder != taker:
+                            other = taken[(taker - holder) % 4 - 1, unit * UNIT:(unit + 1) * UNIT]
+                            value = jnp.where(kept[rank] // 2 == holder, other, value)
+                    compact[0, unit * UNIT:(unit + 1) * UNIT] = value
 
     def lhs(i, first, core):
         loaded = arrived[i, first:first + 2, :, core]
@@ -246,6 +318,8 @@
     def multiply(i):
         f_copy(i, 0, far_t).wait_recv()
         f_copy(i, 1, far_t).wait_recv()
+        y_copy(i, 0, 1, up_t).wait_recv()
+        y_copy(i, 1, 0, down_t).wait_recv()
         low, high = lhs(i, 0, 0), lhs(i, 0, 1)
         grad_low, grad_high = lhs(i, 2, 0), lhs(i, 2, 1)
 
@@ -275,43 +349,60 @@
             r_copy(i, k, (p + 4 - k) % 4).wait_recv()
             total = total + sums[i, (p + 4 - k) % 4]
         hidden = total[0] / (1.0 + jnp.exp(-total[0])) * total[1]
-        products[i] = hidden * total[2]
-
-    for copy in copies:
+        local(gate_send.at[e], gate_recv.at[i], g_recv.at[i]).wait()
+        column = jnp.sum(
+            jnp.where(row24 == lane24, jnp.broadcast_to(gate_recv[i], (8 * CAP, 128)), 0.0), axis=1, keepdims=True
+        )
+        acc[...] += column * hidden * total[2]
+
+    for copy in copies[:2]:
         copy.wait()
-
-    def step(s, carry):
-        @pl.when((s >= 1) & (s < steps + 1))
-        def _():
-            take_y(s - 1)
-
-        @pl.when(s < steps)
-        def _():
-            take_z(s)
-
-        @pl.when((s >= 1) & (s < steps + 1))
-        def _():
-            multiply(s - 1)
-
-        @pl.when(s >= 2)
-        def _():
-            finish(s - 2)
-        return carry
-
-    lax.fori_loop(0, steps + 2, step, 0)
-
     row24 = lax.broadcasted_iota(jnp.int32, (8 * CAP, 128), 0)
     lane24 = lax.broadcasted_iota(jnp.int32, (8 * CAP, 128), 1)
-
-    def weigh(i, total):
-        local(gate_send.at[e], gate_recv.at[i], g_recv.at[i]).wait()
-        line = gate_recv[i]
-        column = jnp.sum(
-            jnp.where(row24 == lane24, jnp.broadcast_to(line[0:1], (8 * CAP, 128)), 0.0), axis=1, keepdims=True
-        )
-        return total + column * products[i]
-
-    total = lax.fori_loop(0, steps, weigh, jnp.zeros((8 * CAP, products.shape[2]), jnp.float32))
+    acc[...] = jnp.zeros(acc.shape, jnp.float32)
+    take_z(steps - 1, 0)
+
+    def step(s, carry):
+        @pl.when(s == 1)
+        def _():
+            take_y(steps - 1, 0)
+
+        @pl.when((s >= 1) & (s < steps))
+        def _():
+            take_y(s - 1, 0)
+
+        @pl.when((s >= 1) & (s < steps + 1))
+        def _():
+            take_y(s - 1, 1)
+
+        @pl.when(s < steps - 1)
+        def _():
+            take_z(s, 0)
+
+        @pl.when(s < steps)
+        def _():
+            take_z(s, 1)
+
+        @pl.when(s < steps - WINDOW)
+        def _():
+            z_sent(s)
+            z_start(s + WINDOW, 0)
+
+        @pl.when((s >= 1) & (s < steps + 1))
+        def _():
+            multiply(s - 1)
+
+        @pl.when(s >= 2)
+        def _():
+            finish(s - 2)
+
+        @pl.when(s == steps // 2)
+        def _():
+            take_compact()
+        return carry
+
+    lax.fori_loop(0, steps + 2, step, 0)
+    total = acc[...]
     share[...] = jnp.broadcast_to(jnp.sum(total, axis=0, keepdims=True), share.shape)
     shares[p] = share[...]
 
@@ -332,17 +423,16 @@
         raw_copy(k, (b + k) % 8, b).wait_send()
     g_each(lambda copy: copy.wait_send())
 
+    each_offer(lambda copy: copy.wait_send())
+
     def drain(i, carry):
-        for sign in range(2):
-            for core in range(2):
-                if sign == 1:
-                    z_copy(i, 1, core, c).wait_send()
-                else:
-                    @pl.when((i != steps - 1) | (c != core))
-                    def _():
-                        z_copy(i, 0, core, c).wait_send()
+        @pl.when(i >= steps - WINDOW)
+        def _():
+            z_sent(i)
+
         for way in range(2):
-            y_copy(i, way, t).wait_send()
+            for sign in range(2):
+                y_copy(i, sign, way, t).wait_send()
             f_copy(i, way, down_t if way == 0 else up_t).wait_send()
         for k in range(1, 4):
             r_copy(i, k, p).wait_send()
@@ -351,75 +441,63 @@
     lax.fori_loop(0, steps, drain, 0)
 
 
-def routed(tokens, cotangent, info, gate_weight, up_weight, down_weight, experts):
+def routed(tokens, cotangent, routes, route_gate, dropped, gate_weight, up_weight, down_weight, experts):
     steps = experts // 4
     rows, width = tokens.shape[1:]
     lanes = width // 8
     depth, columns = gate_weight.shape[1:]
     slab = CAP
-    anywhere = pl.BlockSpec(memory_space=pl.ANY)
+    anywhere = pl.BlockSpec(memory_space=pltpu.HBM)
     vmem = pl.BlockSpec(memory_space=pltpu.VMEM)
     half, full, dma = jnp.bfloat16, jnp.float32, pltpu.SemaphoreType.DMA
     return pl.pallas_call(
         functools.partial(kernel, experts),
-        out_shape=jax.ShapeDtypeStruct((2, 8, columns), full),
-        in_specs=[anywhere, anywhere, vmem, anywhere, anywhere, anywhere],
-        out_specs=vmem,
+        out_shape=(
+            jax.ShapeDtypeStruct((2, 1, columns), full),
+            jax.ShapeDtypeStruct((1, KEEP * UNIT, depth), half),
+        ),
+        in_specs=[anywhere] * 4 + [pl.BlockSpec(memory_space=pltpu.SMEM)] + [anywhere] * 3,
+        out_specs=(vmem, vmem),
         scratch_shapes=[
             pltpu.VMEM((rows, width), half),
+            pltpu.VMEM((2, 2, rows), jnp.int32),
+            pltpu.VMEM((2, 2, rows), half),
             pltpu.VMEM((8, rows, lanes), half),
             pltpu.VMEM((2, 8, 128), full),
             pltpu.VMEM((8, 2, 8, 128), full),
             pltpu.VMEM((experts * slab, 8, lanes), half),
-            pltpu.VMEM((experts, 8, 128), full),
-            pltpu.VMEM((steps, 8, 128), full),
+            pltpu.VMEM((experts, 1, 128), full),
+            pltpu.VMEM((steps, 1, 128), full),
             pltpu.VMEM((steps, 4, 2, 2, slab, 8, lanes), half),
             pltpu.VMEM((depth, columns), half),
             pltpu.VMEM((depth, columns), half),
             pltpu.VMEM((columns, depth), half),
             pltpu.VMEM((steps, 4, 3, 8 * CAP, columns), full),
             pltpu.VMEM((steps, 4, 3, 8 * CAP, columns), full),
-            pltpu.VMEM((steps, 8 * CAP, columns), full),
-            pltpu.VMEM((8, columns), full),
-            pltpu.VMEM((4, 8, columns), full),
-            dma((5,)),
+            pltpu.VMEM((8 * CAP, columns), full),
+            pltpu.VMEM((1, columns), full),
+            pltpu.VMEM((4, 1, columns), full),
+            pltpu.VMEM((KEEP * BLOCK, depth), half),
+            pltpu.VMEM((3, KEEP * UNIT, depth), half),
+            dma((7,)),
             dma((8,)), dma((8,)), dma((8,)), dma((8,)),
             dma((steps, 2, 2)), dma((steps, 2, 2)),
             dma((steps, 2)), dma((steps,)),
-            dma((steps, 2)), dma((steps, 2)), dma((steps, 2)), dma((steps, 2)),
-            dma((steps, 3)), dma((steps, 3)), dma((3,)), dma((3,)),
+            dma((steps, 2, 2)), dma((steps, 2, 2)), dma((steps, 2)), dma((steps, 2)),
+            dma((steps, 3)), dma((steps, 3)), dma((3,)), dma((3,)), dma((3,)), dma((3,)),
         ],
         compiler_params=pltpu.CompilerParams(
             collective_id=0, has_side_effects=True, vmem_limit_bytes=40 * 1024 * 1024
         ),
         cost_estimate=pl.CostEstimate(flops=4 * 10**9, transcendentals=10**5, bytes_accessed=2 * 10**8),
-    )(tokens, cotangent, info, gate_weight, up_weight, down_weight)
-
-
-def compaction(down_weight, dropped, tensor_pos, tensor_count):
-    blocks = jnp.arange(NBLK, dtype=jnp.int32)
-    kept_flag = jnp.all(dropped[0][:, None] != blocks[None, :], axis=0)
-    ranking = jnp.cumsum(kept_flag.astype(jnp.int32)) - 1
-    rows_out = KEEP * BLOCK // tensor_count
-    whole_rows = lax.all_gather(down_weight, "tensor", axis=1, tiled=True)[0]
-    target_rows = tensor_pos * rows_out + jnp.arange(rows_out, dtype=jnp.int32)
-    wanted_rank = target_rows // BLOCK
-    chosen_block = kept_flag[None, :] & (ranking[None, :] == wanted_rank[:, None])
-    source_block = jnp.sum(jnp.where(chosen_block, blocks[None, :], 0), axis=1)
-    source_rows = source_block * BLOCK + target_rows % BLOCK
-    return jnp.take(whole_rows, source_rows, axis=0)[None]
+    )(tokens, cotangent, routes, route_gate, dropped, gate_weight, up_weight, down_weight)
 
 
 def body(tokens, cotangent, route_gate, routes, gate_weight, up_weight, down_weight, dropped):
-    experts = lax.axis_size("expert")
-    tensor_count = lax.axis_size("tensor")
-    tensor_pos = lax.axis_index("tensor")
-    lines = jnp.concatenate([routes.astype(jnp.float32), route_gate.astype(jnp.float32)], axis=2)
-    lines = jnp.transpose(lines, (0, 2, 1))
-    info = jnp.pad(jnp.tile(lines, (1, 1, 4)), ((0, 0), (0, 4), (0, 0)))
-    values = routed(tokens, cotangent, info, gate_weight, up_weight, down_weight, experts)
-    saliency = values[:, :1]
-    return (saliency, compaction(down_weight, dropped, tensor_pos, tensor_count))
+    return routed(
+        tokens, cotangent, jnp.transpose(routes, (0, 2, 1)), jnp.transpose(route_gate, (0, 2, 1)), dropped,
+        gate_weight, up_weight, down_weight, lax.axis_size("expert"),
+    )
 
 
 def solution(mesh):

time: 145 us -> 119 us (0.82)
  the two profiles are of different devices: /device:TPU:8 before, /device:TPU:32 now
where the time goes in v3:
time: 119 us; the launch traced here: 118 us
  Pallas kernels  110 us (92%)
  local copies, waits for them, and re-layouts  7.96 us (7%)
    pallas_call x1, Pallas kernels, routed(): pl.pallas_call(functools.partial(kernel, experts), out_shape=(jax.ShapeDt...  110 us
    unnamed x18, local copies, waits for them, and re-layouts  7.96 us

profile of v3, /device:TPU:32, one launch (start us, length us, event | category | flops | bytes accessed | tf_op | source)
XLA Modules:
  0.0 118.2 jit_solution(3047593169801571193)
XLA Ops:
  0.6 0.0 copy-start.5
  0.6 0.0 copy-start.6
  0.7 0.0 copy-start.7
  0.7 0.7 copy-done.5
  1.3 0.0 copy-done.6
  1.3 0.0 copy-done.7
  1.3 0.0 copy-start
  1.3 1.2 copy-done
  2.5 0.0 copy-start.1
  2.5 1.2 copy-done.1
  3.7 0.0 copy-start.2
  3.7 1.2 copy-done.2
  4.9 0.0 copy-start.3
  4.9 1.2 copy-done.3
  6.0 0.0 copy-start.4
  6.1 1.2 copy-done.4
  7.2 109.6 %shard_map.95 = (f32[2,1,256]{2,1,0:T(1,128)S(1)}, bf16[1,160,1792]{2,1,0:T(8,128)(2,1)S(1)}) custom-call(bf16[2,32,7168]{2,1,0:T(8,128)(2,1)S(1)} %copy-done, bf16[2,32,7168]{2,1,0:T(8,128)(2,1)S(1)} %copy-done.1, s32[2,2,32]{2,1,0:T(2,128)S(1)} %bitcast.2, bf16[2,2,32]{2,1,0:T(2,128)(2,1)S(1)} %bitcast.3, s32[1,3]{1,0:T(1,128)S(1)} %copy-done.7, ...), custom_call_target="tpu_custom_call" | custom-call | flops 4000000000 | bytes 200000000 | tf_op jit(solution)/shard_map/pallas_call | solution.py:453
  116.8 0.6 copy.12
  117.4 0.8 copy.13
Async XLA Ops:
  0.6 0.7 copy-start.5
  0.6 0.7 copy-start.6
  0.7 0.7 copy-start.7
  1.3 1.2 copy-start
  2.5 1.2 copy-start.1
  3.7 1.2 copy-start.2
  4.9 1.2 copy-start.3
  6.0 1.2 copy-start.4

commit v4 on v3

--- a/solution.py
+++ b/solution.py
@@ -20,8 +20,8 @@
 def kernel(
     experts,
     tokens, cotangent, routes, route_gate, dropped, gate_w, up_w, down_w,
-    out, compact,
-    mine, own_routes, own_gates, raw, info_own, info_all, packed, gate_send, gate_recv, arrived, wg, wu, wd, partial, sums, acc, share, shares, offered, taken,
+    out, compact_out,
+    mine, own_routes, own_gates, raw, info_own, info_all, packed, gate_send, gate_recv, arrived, wg, wu, wd, wdt, partial, sums, acc, share, shares, offered, taken, compact,
     local_sem, raw_send, raw_recv, info_send, info_recv, z_send, z_recv, g_send, g_recv,
     y_send, y_recv, f_send, f_recv, r_send, r_recv, s_send, s_recv, c_send, c_recv,
 ):
@@ -47,6 +47,23 @@
             device_id={"expert": expert, "dp": dp, "tensor": tensor}, device_id_type=MESH,
         )
 
+    barrier = pltpu.get_barrier_semaphore()
+
+    def greet(expert, dp, tensor):
+        pl.semaphore_signal(
+            barrier, inc=1, device_id={"expert": expert, "dp": dp, "tensor": tensor}, device_id_type=MESH
+        )
+
+    def greet_z(k, carry):
+        greet((e + k) % experts, p, t)
+        return carry
+
+    lax.fori_loop(1, experts, greet_z, 0)
+    for k in range(1, 4):
+        greet(e, (p + k) % 4, t)
+        greet(2 * z + 1 - c, (p + k) % 4, t)
+        greet(e, p, (t + k) % 4)
+
     for index in range(4):
         source = tokens if index < 2 else cotangent
 
@@ -61,23 +78,6 @@
         copy.start()
     for copy in copies:
         copy.start()
-
-    barrier = pltpu.get_barrier_semaphore()
-
-    def greet(expert, dp, tensor):
-        pl.semaphore_signal(
-            barrier, inc=1, device_id={"expert": expert, "dp": dp, "tensor": tensor}, device_id_type=MESH
-        )
-
-    def greet_z(k, carry):
-        greet((e + k) % experts, p, t)
-        return carry
-
-    lax.fori_loop(1, experts, greet_z, 0)
-    for k in range(1, 4):
-        greet(e, (p + k) % 4, t)
-        greet(2 * z + 1 - c, (p + k) % 4, t)
-        greet(e, p, (t + k) % 4)
 
     for copy in small:
         copy.wait()
@@ -92,6 +92,27 @@
             wide = jnp.dot(lines.astype(jnp.bfloat16), spread_of, preferred_element_type=jnp.float32)
             info_own[which, at:at + 2] = jnp.where(own_lanes, wide, 0.0)
     info_all[b] = info_own[...]
+    local(tokens.at[0], mine, local_sem.at[0]).wait()
+    pl.semaphore_wait(barrier, experts - 1 + 9)
+
+    def raw_copy(k, other, owner):
+        return remote(
+            mine.at[:, pl.ds(pl.multiple_of(other * lanes, 128), lanes)], raw.at[owner],
+            raw_send.at[k], raw_recv.at[k], 2 * z + other % 2, other // 2, t,
+        )
+
+    def info_copy(k, other, owner):
+        return remote(
+            info_own, info_all.at[owner], info_send.at[k], info_recv.at[k], 2 * z + other % 2, other // 2, t
+        )
+
+    own_raw = local(mine.at[:, pl.ds(pl.multiple_of(b * lanes, 128), lanes)], raw.at[b], local_sem.at[4])
+    own_raw.start()
+    for k in range(1, 8):
+        info_copy(k, (b + k) % 8, b).start()
+    for k in range(1, 8):
+        raw_copy(k, (b + k) % 8, b).start()
+
     first, second, third = dropped[0, 0], dropped[0, 1], dropped[0, 2]
     least = jnp.minimum(first, jnp.minimum(second, third))
     most = jnp.maximum(first, jnp.maximum(second, third))
@@ -104,26 +125,6 @@
     copies[2].wait()
     for rank in range(KEEP):
         offered[rank * BLOCK:(rank + 1) * BLOCK] = jnp.where(kept[rank] == 2 * t, wd[:BLOCK], wd[BLOCK:])
-    local(tokens.at[0], mine, local_sem.at[0]).wait()
-    pl.semaphore_wait(barrier, experts - 1 + 9)
-
-    def raw_copy(k, other, owner):
-        return remote(
-            mine.at[:, pl.ds(pl.multiple_of(other * lanes, 128), lanes)], raw.at[owner],
-            raw_send.at[k], raw_recv.at[k], 2 * z + other % 2, other // 2, t,
-        )
-
-    def info_copy(k, other, owner):
-        return remote(
-            info_own, info_all.at[owner], info_send.at[k], info_recv.at[k], 2 * z + other % 2, other // 2, t
-        )
-
-    own_raw = local(mine.at[:, pl.ds(pl.multiple_of(b * lanes, 128), lanes)], raw.at[b], local_sem.at[4])
-    own_raw.start()
-    for k in range(1, 8):
-        info_copy(k, (b + k) % 8, b).start()
-    for k in range(1, 8):
-        raw_copy(k, (b + k) % 8, b).start()
 
     def offer(holder, taker, start, size):
         away = (taker - holder) % 4 - 1
@@ -276,10 +277,21 @@
             e, p, up_t if way == 0 else down_t,
         )
 
+    def far_copy(i):
+        return remote(
+            arrived.at[i, t, 1], arrived.at[i, t, 1], f_send.at[i, 1], f_recv.at[i, 1], e, p, far_t
+        )
+
     def r_copy(i, k, owner):
         other = (p + k) % 4
         return remote(
             partial.at[i, other], sums.at[i, owner], r_send.at[i, k - 1], r_recv.at[i, k - 1], e, other, t
+        )
+
+    def r_part(i, k, index):
+        other = (p + k) % 4
+        return remote(
+            partial.at[i, other, index], sums.at[i, p, index], r_send.at[i, k - 1], r_recv.at[i, k - 1], e, other, t
         )
 
     def take_z(i, sign):
@@ -287,11 +299,20 @@
             z_copy(i, sign, core, core).wait_recv()
         y_copy(i, sign, 0, t).start()
         y_copy(i, sign, 1, t).start()
+        if sign == 1:
+            @pl.when(i == steps - 1)
+            def _():
+                far_copy(i).start()
 
     def take_y(i, sign):
         owner = down_t if sign == 0 else up_t
         y_copy(i, sign, sign, owner).wait_recv()
-        f_copy(i, sign, owner).start()
+        if sign == 0:
+            f_copy(i, sign, owner).start()
+        else:
+            @pl.when(i != steps - 1)
+            def _():
+                f_copy(i, sign, owner).start()
 
     def take_compact():
         for entry in OFFERS:
@@ -309,7 +330,7 @@
                         if holder != taker:
                             other = taken[(taker - holder) % 4 - 1, unit * UNIT:(unit + 1) * UNIT]
                             value = jnp.where(kept[rank] // 2 == holder, other, value)
-                    compact[0, unit * UNIT:(unit + 1) * UNIT] = value
+                    compact[unit * UNIT:(unit + 1) * UNIT] = value
 
     def lhs(i, first, core):
         loaded = arrived[i, first:first + 2, :, core]
@@ -323,25 +344,19 @@
         low, high = lhs(i, 0, 0), lhs(i, 0, 1)
         grad_low, grad_high = lhs(i, 2, 0), lhs(i, 2, 1)
 
-        def plain(weight):
-            return jnp.dot(low, weight[:lanes], preferred_element_type=jnp.float32) + jnp.dot(
-                high, weight[lanes:], preferred_element_type=jnp.float32
+        def product(one, two, weight):
+            return jnp.dot(one, weight[:lanes], preferred_element_type=jnp.float32) + jnp.dot(
+                two, weight[lanes:], preferred_element_type=jnp.float32
             )
 
-        turned = (((1,), (1,)), ((), ()))
-        results = (
-            plain(wg),
-            plain(wu),
-            lax.dot_general(grad_low, wd[:, :lanes], turned, preferred_element_type=jnp.float32)
-            + lax.dot_general(grad_high, wd[:, lanes:], turned, preferred_element_type=jnp.float32),
-        )
-        for index, value in enumerate(results):
+        for index, (one, two, weight) in enumerate(((low, high, wg), (low, high, wu), (grad_low, grad_high, wdt))):
+            value = product(one, two, weight)
             for which in range(2):
                 for sign in range(2):
                     at = (2 * which + sign) * 8 * CAP
                     partial[i, 2 * sign + which, index] = value[at:at + 8 * CAP]
-        for k in range(1, 4):
-            r_copy(i, k, p).start()
+            for k in range(1, 4):
+                r_part(i, k, index).start()
 
     def finish(i):
         total = partial[i, p]
@@ -360,6 +375,7 @@
     row24 = lax.broadcasted_iota(jnp.int32, (8 * CAP, 128), 0)
     lane24 = lax.broadcasted_iota(jnp.int32, (8 * CAP, 128), 1)
     acc[...] = jnp.zeros(acc.shape, jnp.float32)
+    wdt[...] = jnp.transpose(wd[...].astype(jnp.float32)).astype(jnp.bfloat16)
     take_z(steps - 1, 0)
 
     def step(s, carry):
@@ -399,6 +415,7 @@
         @pl.when(s == steps // 2)
         def _():
             take_compact()
+            local(compact, compact_out.at[0], local_sem.at[1]).start()
         return carry
 
     lax.fori_loop(0, steps + 2, step, 0)
@@ -424,6 +441,7 @@
     g_each(lambda copy: copy.wait_send())
 
     each_offer(lambda copy: copy.wait_send())
+    local(compact, compact_out.at[0], local_sem.at[1]).wait()
 
     def drain(i, carry):
         @pl.when(i >= steps - WINDOW)
@@ -457,7 +475,7 @@
             jax.ShapeDtypeStruct((1, KEEP * UNIT, depth), half),
         ),
         in_specs=[anywhere] * 4 + [pl.BlockSpec(memory_space=pltpu.SMEM)] + [anywhere] * 3,
-        out_specs=(vmem, vmem),
+        out_specs=(vmem, anywhere),
         scratch_shapes=[
             pltpu.VMEM((rows, width), half),
             pltpu.VMEM((2, 2, rows), jnp.int32),
@@ -472,6 +490,7 @@
             pltpu.VMEM((depth, columns), half),
             pltpu.VMEM((depth, columns), half),
             pltpu.VMEM((columns, depth), half),
+            pltpu.VMEM((depth, columns), half),
             pltpu.VMEM((steps, 4, 3, 8 * CAP, columns), full),
             pltpu.VMEM((steps, 4, 3, 8 * CAP, columns), full),
             pltpu.VMEM((8 * CAP, columns), full),
@@ -479,6 +498,7 @@
             pltpu.VMEM((4, 1, columns), full),
             pltpu.VMEM((KEEP * BLOCK, depth), half),
             pltpu.VMEM((3, KEEP * UNIT, depth), half),
+            pltpu.VMEM((KEEP * UNIT, depth), half),
             dma((7,)),
             dma((8,)), dma((8,)), dma((8,)), dma((8,)),
             dma((steps, 2, 2)), dma((steps, 2, 2)),
@@ -487,7 +507,7 @@
             dma((steps, 3)), dma((steps, 3)), dma((3,)), dma((3,)), dma((3,)), dma((3,)),
         ],
         compiler_params=pltpu.CompilerParams(
-            collective_id=0, has_side_effects=True, vmem_limit_bytes=40 * 1024 * 1024
+            collective_id=0, has_side_effects=True, vmem_limit_bytes=62 * 1024 * 1024
         ),
         cost_estimate=pl.CostEstimate(flops=4 * 10**9, transcendentals=10**5, bytes_accessed=2 * 10**8),
     )(tokens, cotangent, routes, route_gate, dropped, gate_weight, up_weight, down_weight)

time: 119 us -> 113 us (0.950)
  local copies, waits for them, and re-layouts: 7.96 us -> 3.15 us
    unnamed x18 -> x4, local copies, waits for them, and re-layouts: 7.96 us -> 3.15 us
where the time goes in v4:
time: 113 us
  Pallas kernels  109 us (96%)
  local copies, waits for them, and re-layouts  3.15 us (3%)
    pallas_call x1, Pallas kernels, routed(): pl.pallas_call(functools.partial(kernel, experts), out_shape=(jax.ShapeDt...  109 us
    unnamed x4, local copies, waits for them, and re-layouts  3.15 us

profile of v4, /device:TPU:32, one launch (start us, length us, event | category | flops | bytes accessed | tf_op | source)
XLA Modules:
  0.0 112.5 jit_solution(12075577616000778065)
XLA Ops:
  0.6 108.7 %shard_map.95 = (f32[2,1,256]{2,1,0:T(1,128)}, bf16[1,160,1792]{2,1,0:T(8,128)(2,1)}) custom-call(bf16[2,32,7168]{2,1,0:T(8,128)(2,1)} %tokens.1, bf16[2,32,7168]{2,1,0:T(8,128)(2,1)} %cotangent.1, s32[2,2,32]{2,1,0:T(2,128)} %bitcast.2, bf16[2,2,32]{2,1,0:T(2,128)(2,1)} %bitcast.3, s32[1,3]{1,0:T(1,128)} %dropped.1, bf16[1,1792,256]{2,1,0:T(8,128)(2,1)} %gate_w.1, ...), custom_call_target="tpu_custom_call" | custom-call | flops 4000000000 | bytes 200000000 | tf_op jit(solution)/shard_map/pallas_call | solution.py:471
  109.4 0.0 copy-start
  109.4 0.7 copy-done
  110.1 0.6 copy.12
  110.6 1.9 %copy.13 = bf16[1,160,1792]{2,1,0:T(8,128)(2,1)} copy(bf16[1,160,1792]{2,1,0:T(8,128)(2,1)} %get-tuple-element.5) | data formatting | bytes 1146880
Async XLA Ops:
  109.4 0.7 copy-start

commit v5 on v4

--- a/solution.py
+++ b/solution.py
@@ -12,16 +12,17 @@
 CAP = 3
 MESH = pl.DeviceIdType.MESH
 UNIT = 32
-WINDOW = 3
+WINDOW = 4
+AHEAD = 384
 OFFERS = ((0, 1, 5, 3), (1, 0, 0, 5), (1, 2, 10, 5), (1, 3, 15, 1), (2, 0, 4, 1), (2, 1, 5, 5), (2, 3, 15, 5), (3, 2, 12, 3))
 HOLDERS = ((0, 1), (0, 1, 2), (1, 2), (1, 2, 3), (2, 3))
 
 
 def kernel(
     experts,
-    tokens, cotangent, routes, route_gate, dropped, gate_w, up_w, down_w,
+    tokens, cotangent, routes, route_gate, dropped_in, gate_w, up_w, down_w,
     out, compact_out,
-    mine, own_routes, own_gates, raw, info_own, info_all, packed, gate_send, gate_recv, arrived, wg, wu, wd, wdt, partial, sums, acc, share, shares, offered, taken, compact,
+    mine, own_routes, own_gates, dropped, raw, info_own, info_all, packed, gate_send, gate_recv, arrived, wg, wu, wd, wdt, partial, sums, acc, share, shares, offered, taken, compact,
     local_sem, raw_send, raw_recv, info_send, info_recv, z_send, z_recv, g_send, g_recv,
     y_send, y_recv, f_send, f_recv, r_send, r_recv, s_send, s_recv, c_send, c_recv,
 ):
@@ -76,6 +77,7 @@
     small = [local(routes, own_routes, local_sem.at[5]), local(route_gate, own_gates, local_sem.at[6])]
     for copy in small:
         copy.start()
+    local(dropped_in, dropped, local_sem.at[7]).start()
     for copy in copies:
         copy.start()
 
@@ -95,10 +97,13 @@
     local(tokens.at[0], mine, local_sem.at[0]).wait()
     pl.semaphore_wait(barrier, experts - 1 + 9)
 
-    def raw_copy(k, other, owner):
-        return remote(
-            mine.at[:, pl.ds(pl.multiple_of(other * lanes, 128), lanes)], raw.at[owner],
-            raw_send.at[k], raw_recv.at[k], 2 * z + other % 2, other // 2, t,
+    parts = ((0, AHEAD), (AHEAD, lanes - AHEAD))
+
+    def raw_copy(part, k, other, owner):
+        start, size = parts[part]
+        return remote(
+            mine.at[:, pl.ds(pl.multiple_of(other * lanes + start, 128), size)], raw.at[owner, :, pl.ds(start, size)],
+            raw_send.at[part, k], raw_recv.at[part, k], 2 * z + other % 2, other // 2, t,
         )
 
     def info_copy(k, other, owner):
@@ -111,8 +116,9 @@
     for k in range(1, 8):
         info_copy(k, (b + k) % 8, b).start()
     for k in range(1, 8):
-        raw_copy(k, (b + k) % 8, b).start()
-
+        raw_copy(0, k, (b + k) % 8, b).start()
+
+    local(dropped_in, dropped, local_sem.at[7]).wait()
     first, second, third = dropped[0, 0], dropped[0, 1], dropped[0, 2]
     least = jnp.minimum(first, jnp.minimum(second, third))
     most = jnp.maximum(first, jnp.maximum(second, third))
@@ -140,6 +146,8 @@
                 act(offer(*entry))
 
     each_offer(lambda copy: copy.start())
+    for k in range(1, 8):
+        raw_copy(1, k, (b + k) % 8, b).start()
     for k in range(1, 8):
         info_copy(k, (b + k) % 8, (b + 8 - k) % 8).wait_recv()
 
@@ -174,14 +182,19 @@
         return jnp.where(jnp.broadcast_to(part[:, None, :], slot_of.shape) == slot_of, 1.0, 0.0)
 
     place, _ = places(t % 2)
-    for k in range(1, 8):
-        raw_copy(k, (b + k) % 8, (b + 8 - k) % 8).wait_recv()
     own_raw.wait()
-    whole = raw[...].reshape(count, lanes)
-    for start in range(0, experts, group):
-        select = chosen_rows(place, start).reshape(group * 8 * CAP, count).astype(jnp.bfloat16)
-        values = jnp.dot(select, whole, preferred_element_type=jnp.float32)
-        packed[slab * start:slab * (start + group)] = values.reshape(slab * group, 8, lanes).astype(jnp.bfloat16)
+
+    def pack(part):
+        start, size = parts[part]
+        for k in range(1, 8):
+            raw_copy(part, k, (b + k) % 8, (b + 8 - k) % 8).wait_recv()
+        whole = raw[:, :, start:start + size].reshape(count, size)
+        for first_expert in range(0, experts, group):
+            select = chosen_rows(place, first_expert).reshape(group * 8 * CAP, count).astype(jnp.bfloat16)
+            values = jnp.dot(select, whole, preferred_element_type=jnp.float32)
+            packed[slab * first_expert:slab * (first_expert + group), :, start:start + size] = values.reshape(
+                slab * group, 8, size
+            ).astype(jnp.bfloat16)
 
     def plane(i, sign):
         return (z + (i + 1 if sign else planes - (i + 1) % steps)) % planes
@@ -193,16 +206,34 @@
             z_send.at[i, sign, core], z_recv.at[i, sign, owner_core], expert, p, t,
         )
 
+    def z_part(i, sign, core, part):
+        expert = 2 * plane(i, sign) + core
+        span = pl.ds(*parts[part])
+        return remote(
+            packed.at[pl.ds(expert * slab, slab), :, span], arrived.at[i, t, sign, c, :, :, span],
+            z_send.at[i, sign, core], z_recv.at[i, sign, c], expert, p, t,
+        )
+
     def z_start(i, carry):
-        for sign in range(2):
+        for core in range(2):
+            z_copy(i, 1, core, c).start()
+
+            @pl.when(i != steps - 1)
+            def _():
+                z_copy(i, 0, core, c).start()
+        return carry
+
+    window = min(WINDOW, steps - 1)
+    for part in range(2):
+        pack(part)
+
+        def z_begin(i, carry):
             for core in range(2):
-                if sign == 1:
-                    z_copy(i, 1, core, c).start()
-                else:
-                    @pl.when(i != steps - 1)
-                    def _():
-                        z_copy(i, 0, core, c).start()
-        return carry
+                for sign in (1, 0):
+                    z_part(i, sign, core, part).start()
+            return carry
+
+        lax.fori_loop(0, window, z_begin, 0)
 
     def z_sent(i):
         for sign in range(2):
@@ -220,7 +251,6 @@
         @pl.when(c != core)
         def _():
             z_copy(steps - 1, 0, core, c).start()
-    lax.fori_loop(0, min(WINDOW, steps), z_start, 0)
 
     gate_place, gate_weight = places(p % 2)
     row_at = lax.broadcasted_iota(jnp.int32, (group, 8 * CAP, 128), 1)
@@ -399,10 +429,10 @@
         def _():
             take_z(s, 1)
 
-        @pl.when(s < steps - WINDOW)
+        @pl.when(s < steps - window)
         def _():
             z_sent(s)
-            z_start(s + WINDOW, 0)
+            z_start(s + window, 0)
 
         @pl.when((s >= 1) & (s < steps + 1))
         def _():
@@ -437,14 +467,15 @@
         s_copy(k, p).wait_send()
     for k in range(1, 8):
         info_copy(k, (b + k) % 8, b).wait_send()
-        raw_copy(k, (b + k) % 8, b).wait_send()
+        for part in range(2):
+            raw_copy(part, k, (b + k) % 8, b).wait_send()
     g_each(lambda copy: copy.wait_send())
 
     each_offer(lambda copy: copy.wait_send())
     local(compact, compact_out.at[0], local_sem.at[1]).wait()
 
     def drain(i, carry):
-        @pl.when(i >= steps - WINDOW)
+        @pl.when(i >= steps - window)
         def _():
             z_sent(i)
 
@@ -474,12 +505,13 @@
             jax.ShapeDtypeStruct((2, 1, columns), full),
             jax.ShapeDtypeStruct((1, KEEP * UNIT, depth), half),
         ),
-        in_specs=[anywhere] * 4 + [pl.BlockSpec(memory_space=pltpu.SMEM)] + [anywhere] * 3,
+        in_specs=[anywhere] * 8,
         out_specs=(vmem, anywhere),
         scratch_shapes=[
             pltpu.VMEM((rows, width), half),
             pltpu.VMEM((2, 2, rows), jnp.int32),
             pltpu.VMEM((2, 2, rows), half),
+            pltpu.SMEM((1, 3), jnp.int32),
             pltpu.VMEM((8, rows, lanes), half),
             pltpu.VMEM((2, 8, 128), full),
             pltpu.VMEM((8, 2, 8, 128), full),
@@ -499,8 +531,8 @@
             pltpu.VMEM((KEEP * BLOCK, depth), half),
             pltpu.VMEM((3, KEEP * UNIT, depth), half),
             pltpu.VMEM((KEEP * UNIT, depth), half),
-            dma((7,)),
-            dma((8,)), dma((8,)), dma((8,)), dma((8,)),
+            dma((8,)),
+            dma((2, 8)), dma((2, 8)), dma((8,)), dma((8,)),
             dma((steps, 2, 2)), dma((steps, 2, 2)),
             dma((steps, 2)), dma((steps,)),
             dma((steps, 2, 2)), dma((steps, 2, 2)), dma((steps, 2)), dma((steps, 2)),

time: 113 us -> 109 us (0.965)
  Pallas kernels: 109 us -> 105 us
    pallas_call x1, Pallas kernels: 109 us -> 105 us  [routed(): pl.pallas_call(functools.partial(kernel, experts), out_shape=(jax.ShapeDt...]
where the time goes in v5:
time: 109 us
  Pallas kernels  105 us (96%)
  local copies, waits for them, and re-layouts  3.15 us (3%)
    pallas_call x1, Pallas kernels, routed(): pl.pallas_call(functools.partial(kernel, experts), out_shape=(jax.ShapeDt...  105 us
    unnamed x4, local copies, waits for them, and re-layouts  3.15 us

profile of v5, /device:TPU:32, one launch (start us, length us, event | category | flops | bytes accessed | tf_op | source)
XLA Modules:
  0.0 109.3 jit_solution(12469633058379185211)
XLA Ops:
  0.6 105.5 %shard_map.95 = (f32[2,1,256]{2,1,0:T(1,128)}, bf16[1,160,1792]{2,1,0:T(8,128)(2,1)}) custom-call(bf16[2,32,7168]{2,1,0:T(8,128)(2,1)} %tokens.1, bf16[2,32,7168]{2,1,0:T(8,128)(2,1)} %cotangent.1, s32[2,2,32]{2,1,0:T(2,128)} %bitcast.2, bf16[2,2,32]{2,1,0:T(2,128)(2,1)} %bitcast.3, s32[1,3]{1,0:T(1,128)} %dropped_in.1, bf16[1,1792,256]{2,1,0:T(8,128)(2,1)} %gate_w.1, ...), custom_call_target="tpu_custom_call" | custom-call | flops 4000000000 | bytes 200000000 | tf_op jit(solution)/shard_map/pallas_call | solution.py:502
  106.1 0.0 copy-start
  106.1 0.7 copy-done
  106.8 0.6 copy.12
  107.4 1.9 %copy.13 = bf16[1,160,1792]{2,1,0:T(8,128)(2,1)} copy(bf16[1,160,1792]{2,1,0:T(8,128)(2,1)} %get-tuple-element.5) | data formatting | bytes 1146880
Async XLA Ops:
  106.1 0.7 copy-start

commit v6 on v5

--- a/solution.py
+++ b/solution.py
@@ -22,9 +22,9 @@
     experts,
     tokens, cotangent, routes, route_gate, dropped_in, gate_w, up_w, down_w,
     out, compact_out,
-    mine, own_routes, own_gates, dropped, raw, info_own, info_all, packed, gate_send, gate_recv, arrived, wg, wu, wd, wdt, partial, sums, acc, share, shares, offered, taken, compact,
+    mine, own_routes, own_gates, dropped, raw, info_own, info_all, packed, gate_send, gate_recv, arrived, wg, wu, wd, wdt, partial, sums, acc, last_part, last_sums, gate_last, share, shares, offered, taken, compact,
     local_sem, raw_send, raw_recv, info_send, info_recv, z_send, z_recv, g_send, g_recv,
-    y_send, y_recv, f_send, f_recv, r_send, r_recv, s_send, s_recv, c_send, c_recv,
+    y_send, y_recv, f_send, f_recv, r_send, r_recv, s_send, s_recv, c_send, c_recv, l_send, l_recv, gl_send, gl_recv,
 ):
     planes = experts // 2
     steps = planes // 2
@@ -271,12 +271,16 @@
             gate_send.at[expert], gate_recv.at[i], g_send.at[i, core], g_recv.at[i], expert, p, t
         )
 
+    def far_gate(core):
+        expert = 2 * plane(steps - 1, 1) + core
+        return remote(gate_send.at[expert], gate_last, gl_send.at[core], gl_recv.at[0], expert, p, t)
+
     own_gate = local(gate_send.at[e], gate_recv.at[steps - 1], g_recv.at[steps - 1])
 
     def g_each(act):
         def g_step(i, carry):
             for core in range(2):
-                @pl.when((c == 0) & (p // 2 == 1))
+                @pl.when((c == 0) & (p // 2 == 1) & (i != steps - 1))
                 def _():
                     act(g_copy(i, 1, core))
 
@@ -286,6 +290,10 @@
             return carry
 
         lax.fori_loop(0, steps, g_step, 0)
+        for core in range(2):
+            @pl.when(c == 0)
+            def _():
+                act(far_gate(core))
 
     g_each(lambda copy: copy.start())
 
@@ -366,6 +374,11 @@
         loaded = arrived[i, first:first + 2, :, core]
         return loaded.astype(jnp.float32).reshape(4 * 8 * CAP, lanes).astype(jnp.bfloat16)
 
+    def product(one, two, weight):
+        return jnp.dot(one, weight[:lanes], preferred_element_type=jnp.float32) + jnp.dot(
+            two, weight[lanes:], preferred_element_type=jnp.float32
+        )
+
     def multiply(i):
         f_copy(i, 0, far_t).wait_recv()
         f_copy(i, 1, far_t).wait_recv()
@@ -373,12 +386,6 @@
         y_copy(i, 1, 0, down_t).wait_recv()
         low, high = lhs(i, 0, 0), lhs(i, 0, 1)
         grad_low, grad_high = lhs(i, 2, 0), lhs(i, 2, 1)
-
-        def product(one, two, weight):
-            return jnp.dot(one, weight[:lanes], preferred_element_type=jnp.float32) + jnp.dot(
-                two, weight[lanes:], preferred_element_type=jnp.float32
-            )
-
         for index, (one, two, weight) in enumerate(((low, high, wg), (low, high, wu), (grad_low, grad_high, wdt))):
             value = product(one, two, weight)
             for which in range(2):
@@ -388,17 +395,74 @@
             for k in range(1, 4):
                 r_part(i, k, index).start()
 
+    def last_copy(k, owner, index):
+        other = (p + k) % 4
+        if index is None:
+            source, target = last_part.at[other], last_sums.at[owner]
+        else:
+            source, target = last_part.at[other, index], last_sums.at[owner, index]
+        return remote(source, target, l_send.at[k - 1], l_recv.at[k - 1], e, other, t)
+
+    def multiply_last(sign):
+        i = steps - 1
+        f_copy(i, sign, far_t).wait_recv()
+        y_copy(i, sign, 1 - sign, down_t if sign else up_t).wait_recv()
+
+        def rows_of(first, core):
+            loaded = arrived[i, first:first + 2, sign, core]
+            return loaded.astype(jnp.float32).reshape(2 * 8 * CAP, lanes).astype(jnp.bfloat16)
+
+        low, high = rows_of(0, 0), rows_of(0, 1)
+        grad_low, grad_high = rows_of(2, 0), rows_of(2, 1)
+        middle = wg.shape[1] // 2
+        for index, (one, two, weight) in enumerate(((low, high, wg), (low, high, wu), (grad_low, grad_high, wdt))):
+            value = product(one, two, weight)
+            for which in range(2):
+                rows_at = value[which * 8 * CAP:(which + 1) * 8 * CAP]
+                if sign == 0:
+                    partial[i, which, index] = rows_at
+                else:
+                    last_part[which, index] = rows_at[:, :middle]
+                    last_part[2 + which, index] = rows_at[:, middle:]
+            for k in range(1, 4):
+                if sign == 0:
+                    @pl.when((p + k) % 4 < 2)
+                    def _():
+                        r_part(i, k, index).start()
+                else:
+                    last_copy(k, p, index).start()
+
     def finish(i):
         total = partial[i, p]
         for k in range(1, 4):
             r_copy(i, k, (p + 4 - k) % 4).wait_recv()
             total = total + sums[i, (p + 4 - k) % 4]
+        local(gate_send.at[e], gate_recv.at[i], g_recv.at[i]).wait()
+        acc[...] += gated(total, gate_recv[i])
+
+    def gated(total, line):
         hidden = total[0] / (1.0 + jnp.exp(-total[0])) * total[1]
-        local(gate_send.at[e], gate_recv.at[i], g_recv.at[i]).wait()
         column = jnp.sum(
-            jnp.where(row24 == lane24, jnp.broadcast_to(gate_recv[i], (8 * CAP, 128)), 0.0), axis=1, keepdims=True
-        )
-        acc[...] += column * hidden * total[2]
+            jnp.where(row24 == lane24, jnp.broadcast_to(line, (8 * CAP, 128)), 0.0), axis=1, keepdims=True
+        )
+        return column * hidden * total[2]
+
+    def finish_last():
+        total = last_part[p]
+        for k in range(1, 4):
+            last_copy(k, (p + 4 - k) % 4, None).wait_recv()
+            total = total + last_sums[(p + 4 - k) % 4]
+        local(gate_send.at[e], gate_last, gl_recv.at[0]).wait()
+        value = gated(total, gate_last[...])
+        middle = wg.shape[1] // 2
+
+        @pl.when(p // 2 == 0)
+        def _():
+            acc[:, :middle] += value
+
+        @pl.when(p // 2 == 1)
+        def _():
+            acc[:, middle:] += value
 
     for copy in copies[:2]:
         copy.wait()
@@ -408,71 +472,12 @@
     wdt[...] = jnp.transpose(wd[...].astype(jnp.float32)).astype(jnp.bfloat16)
     take_z(steps - 1, 0)
 
-    def step(s, carry):
-        @pl.when(s == 1)
-        def _():
-            take_y(steps - 1, 0)
-
-        @pl.when((s >= 1) & (s < steps))
-        def _():
-            take_y(s - 1, 0)
-
-        @pl.when((s >= 1) & (s < steps + 1))
-        def _():
-            take_y(s - 1, 1)
-
-        @pl.when(s < steps - 1)
-        def _():
-            take_z(s, 0)
-
-        @pl.when(s < steps)
-        def _():
-            take_z(s, 1)
-
-        @pl.when(s < steps - window)
-        def _():
-            z_sent(s)
-            z_start(s + window, 0)
-
-        @pl.when((s >= 1) & (s < steps + 1))
-        def _():
-            multiply(s - 1)
-
-        @pl.when(s >= 2)
-        def _():
-            finish(s - 2)
-
-        @pl.when(s == steps // 2)
-        def _():
-            take_compact()
-            local(compact, compact_out.at[0], local_sem.at[1]).start()
-        return carry
-
-    lax.fori_loop(0, steps + 2, step, 0)
-    total = acc[...]
-    share[...] = jnp.broadcast_to(jnp.sum(total, axis=0, keepdims=True), share.shape)
-    shares[p] = share[...]
-
-    def s_copy(k, owner):
-        return remote(share, shares.at[owner], s_send.at[k - 1], s_recv.at[k - 1], e, (p + k) % 4, t)
-
-    for k in range(1, 4):
-        s_copy(k, p).start()
-    for k in range(1, 4):
-        s_copy(k, (p + 4 - k) % 4).wait_recv()
-    out[0] = jnp.abs(shares[0] + shares[2])
-    out[1] = jnp.abs(shares[1] + shares[3])
-
-    for k in range(1, 4):
-        s_copy(k, p).wait_send()
-    for k in range(1, 8):
-        info_copy(k, (b + k) % 8, b).wait_send()
-        for part in range(2):
-            raw_copy(part, k, (b + k) % 8, b).wait_send()
-    g_each(lambda copy: copy.wait_send())
-
-    each_offer(lambda copy: copy.wait_send())
-    local(compact, compact_out.at[0], local_sem.at[1]).wait()
+    def early():
+        for k in range(1, 8):
+            info_copy(k, (b + k) % 8, b).wait_send()
+            for part in range(2):
+                raw_copy(part, k, (b + k) % 8, b).wait_send()
+        g_each(lambda copy: copy.wait_send())
 
     def drain(i, carry):
         @pl.when(i >= steps - window)
@@ -484,10 +489,96 @@
                 y_copy(i, sign, way, t).wait_send()
             f_copy(i, way, down_t if way == 0 else up_t).wait_send()
         for k in range(1, 4):
-            r_copy(i, k, p).wait_send()
+            @pl.when((i != steps - 1) | ((p + k) % 4 < 2))
+            def _():
+                r_copy(i, k, p).wait_send()
         return carry
 
-    lax.fori_loop(0, steps, drain, 0)
+    def step(s, carry):
+        @pl.when(s == 1)
+        def _():
+            take_y(steps - 1, 0)
+
+        @pl.when((s >= 1) & (s < steps))
+        def _():
+            take_y(s - 1, 0)
+
+        @pl.when((s >= 1) & (s < steps + 1))
+        def _():
+            take_y(s - 1, 1)
+
+        @pl.when(s < steps - 1)
+        def _():
+            take_z(s, 0)
+
+        @pl.when(s < steps)
+        def _():
+            take_z(s, 1)
+
+        @pl.when(s < steps - window)
+        def _():
+            z_sent(s)
+            z_start(s + window, 0)
+
+        @pl.when((s >= 1) & (s < steps))
+        def _():
+            multiply(s - 1)
+
+        @pl.when(s == steps)
+        def _():
+            multiply_last(1)
+
+        @pl.when((s >= 2) & (s < steps + 1))
+        def _():
+            finish(s - 2)
+
+        @pl.when(s == 2)
+        def _():
+            early()
+
+        @pl.when(s == 3)
+        def _():
+            multiply_last(0)
+
+        @pl.when((s >= 4) & (s < steps + 1))
+        def _():
+            drain(s - 4, 0)
+
+        @pl.when(s == 6)
+        def _():
+            each_offer(lambda copy: copy.wait_send())
+
+        @pl.when((s == 5) & (p < 2))
+        def _():
+            finish(steps - 1)
+
+        @pl.when(s == steps // 2)
+        def _():
+            take_compact()
+            local(compact, compact_out.at[0], local_sem.at[1]).start()
+        return carry
+
+    lax.fori_loop(0, steps + 1, step, 0)
+    finish_last()
+    total = acc[...]
+    share[...] = jnp.broadcast_to(jnp.sum(total, axis=0, keepdims=True), share.shape)
+    shares[p] = share[...]
+
+    def s_copy(k, owner):
+        return remote(share, shares.at[owner], s_send.at[k - 1], s_recv.at[k - 1], e, (p + k) % 4, t)
+
+    for k in range(1, 4):
+        s_copy(k, p).start()
+    for k in range(1, 4):
+        last_copy(k, p, None).wait_send()
+    local(compact, compact_out.at[0], local_sem.at[1]).wait()
+    lax.fori_loop(steps - 3, steps, drain, 0)
+    for k in range(1, 4):
+        s_copy(k, (p + 4 - k) % 4).wait_recv()
+    out[0] = jnp.abs(shares[0] + shares[2])
+    out[1] = jnp.abs(shares[1] + shares[3])
+    for k in range(1, 4):
+        s_copy(k, p).wait_send()
 
 
 def routed(tokens, cotangent, routes, route_gate, dropped, gate_weight, up_weight, down_weight, experts):
@@ -526,6 +617,9 @@
             pltpu.VMEM((steps, 4, 3, 8 * CAP, columns), full),
             pltpu.VMEM((steps, 4, 3, 8 * CAP, columns), full),
             pltpu.VMEM((8 * CAP, columns), full),
+            pltpu.VMEM((4, 3, 8 * CAP, columns // 2), full),
+            pltpu.VMEM((4, 3, 8 * CAP, columns // 2), full),
+            pltpu.VMEM((1, 128), full),
             pltpu.VMEM((1, columns), full),
             pltpu.VMEM((4, 1, columns), full),
             pltpu.VMEM((KEEP * BLOCK, depth), half),
@@ -537,6 +631,7 @@
             dma((steps, 2)), dma((steps,)),
             dma((steps, 2, 2)), dma((steps, 2, 2)), dma((steps, 2)), dma((steps, 2)),
             dma((steps, 3)), dma((steps, 3)), dma((3,)), dma((3,)), dma((3,)), dma((3,)),
+            dma((3,)), dma((3,)), dma((2,)), dma((1,)),
         ],
         compiler_params=pltpu.CompilerParams(
             collective_id=0, has_side_effects=True, vmem_limit_bytes=62 * 1024 * 1024

time: 109 us -> 108 us (level)
    pallas_call x1, Pallas kernels: 105 us -> 104 us  [routed(): pl.pallas_call(functools.partial(kernel, experts), out_shape=(jax.ShapeDt...]
where the time goes in v6:
time: 108 us
  Pallas kernels  104 us (96%)
  local copies, waits for them, and re-layouts  3.15 us (3%)
    pallas_call x1, Pallas kernels, routed(): pl.pallas_call(functools.partial(kernel, experts), out_shape=(jax.ShapeDt...  104 us
    unnamed x4, local copies, waits for them, and re-layouts  3.15 us

profile of v6, /device:TPU:32, one launch (start us, length us, event | category | flops | bytes accessed | tf_op | source)
XLA Modules:
  0.0 107.7 jit_solution(372591800653843591)
XLA Ops:
  0.6 103.9 %shard_map.95 = (f32[2,1,256]{2,1,0:T(1,128)}, bf16[1,160,1792]{2,1,0:T(8,128)(2,1)}) custom-call(bf16[2,32,7168]{2,1,0:T(8,128)(2,1)} %tokens.1, bf16[2,32,7168]{2,1,0:T(8,128)(2,1)} %cotangent.1, s32[2,2,32]{2,1,0:T(2,128)} %bitcast.2, bf16[2,2,32]{2,1,0:T(2,128)(2,1)} %bitcast.3, s32[1,3]{1,0:T(1,128)} %dropped_in.1, bf16[1,1792,256]{2,1,0:T(8,128)(2,1)} %gate_w.1, ...), custom_call_target="tpu_custom_call" | custom-call | flops 4000000000 | bytes 200000000 | tf_op jit(solution)/shard_map/pallas_call | solution.py:593
  104.6 0.0 copy-start
  104.6 0.7 copy-done
  105.3 0.6 copy.12
  105.8 1.9 %copy.13 = bf16[1,160,1792]{2,1,0:T(8,128)(2,1)} copy(bf16[1,160,1792]{2,1,0:T(8,128)(2,1)} %get-tuple-element.5) | data formatting | bytes 1146880
Async XLA Ops:
  104.6 0.7 copy-start

commit v7 on v6

--- a/solution.py
+++ b/solution.py
@@ -13,7 +13,7 @@
 MESH = pl.DeviceIdType.MESH
 UNIT = 32
 WINDOW = 4
-AHEAD = 384
+AHEAD = 256
 OFFERS = ((0, 1, 5, 3), (1, 0, 0, 5), (1, 2, 10, 5), (1, 3, 15, 1), (2, 0, 4, 1), (2, 1, 5, 5), (2, 3, 15, 5), (3, 2, 12, 3))
 HOLDERS = ((0, 1), (0, 1, 2), (1, 2), (1, 2, 3), (2, 3))
 
@@ -226,6 +226,13 @@
     window = min(WINDOW, steps - 1)
     for part in range(2):
         pack(part)
+        if part == 1:
+            own_slab = local(packed.at[pl.ds(e * slab, slab)], arrived.at[steps - 1, t, 0, c], z_recv.at[steps - 1, 0, c])
+            own_slab.start()
+            for core in range(2):
+                @pl.when(c != core)
+                def _():
+                    z_copy(steps - 1, 0, core, c).start()
 
         def z_begin(i, carry):
             for core in range(2):
@@ -245,25 +252,19 @@
                     def _():
                         z_copy(i, 0, core, c).wait_send()
 
-    own_slab = local(packed.at[pl.ds(e * slab, slab)], arrived.at[steps - 1, t, 0, c], z_recv.at[steps - 1, 0, c])
-    own_slab.start()
-    for core in range(2):
-        @pl.when(c != core)
-        def _():
-            z_copy(steps - 1, 0, core, c).start()
-
-    gate_place, gate_weight = places(p % 2)
-    row_at = lax.broadcasted_iota(jnp.int32, (group, 8 * CAP, 128), 1)
-    lane_at = lax.broadcasted_iota(jnp.int32, (group, 8 * CAP, 128), 2)
-    ones = jnp.ones((count, 128), jnp.bfloat16)
-    for start in range(0, experts, group):
-        part = gate_weight[start:start + group]
-        weighted = chosen_rows(gate_place, start) * jnp.broadcast_to(part[:, None, :], slot_of.shape)
-        spread = jnp.dot(
-            weighted.reshape(group * 8 * CAP, count).astype(jnp.bfloat16), ones, preferred_element_type=jnp.float32
-        ).reshape(group, 8 * CAP, 128)
-        line = jnp.sum(jnp.where(row_at == lane_at, spread, 0.0), axis=1, keepdims=True)
-        gate_send[start:start + group] = line
+    def make_gates():
+        gate_place, gate_weight = places(p % 2)
+        row_at = lax.broadcasted_iota(jnp.int32, (group, 8 * CAP, 128), 1)
+        lane_at = lax.broadcasted_iota(jnp.int32, (group, 8 * CAP, 128), 2)
+        ones = jnp.ones((count, 128), jnp.bfloat16)
+        for start in range(0, experts, group):
+            part = gate_weight[start:start + group]
+            weighted = chosen_rows(gate_place, start) * jnp.broadcast_to(part[:, None, :], slot_of.shape)
+            spread = jnp.dot(
+                weighted.reshape(group * 8 * CAP, count).astype(jnp.bfloat16), ones, preferred_element_type=jnp.float32
+            ).reshape(group, 8 * CAP, 128)
+            line = jnp.sum(jnp.where(row_at == lane_at, spread, 0.0), axis=1, keepdims=True)
+            gate_send[start:start + group] = line
 
     def g_copy(i, sign, core):
         expert = 2 * plane(i, sign) + core
@@ -295,11 +296,12 @@
             def _():
                 act(far_gate(core))
 
-    g_each(lambda copy: copy.start())
-
-    @pl.when((c == 0) & (p // 2 == 0))
-    def _():
-        own_gate.start()
+    def send_gates():
+        g_each(lambda copy: copy.start())
+
+        @pl.when((c == 0) & (p // 2 == 0))
+        def _():
+            own_gate.start()
 
     up_t, down_t, far_t = (t + 1) % 4, (t + 3) % 4, (t + 2) % 4
 
@@ -469,7 +471,6 @@
     row24 = lax.broadcasted_iota(jnp.int32, (8 * CAP, 128), 0)
     lane24 = lax.broadcasted_iota(jnp.int32, (8 * CAP, 128), 1)
     acc[...] = jnp.zeros(acc.shape, jnp.float32)
-    wdt[...] = jnp.transpose(wd[...].astype(jnp.float32)).astype(jnp.bfloat16)
     take_z(steps - 1, 0)
 
     def early():
@@ -514,6 +515,12 @@
         @pl.when(s < steps)
         def _():
             take_z(s, 1)
+
+        @pl.when(s == 0)
+        def _():
+            make_gates()
+            send_gates()
+            wdt[...] = jnp.transpose(wd[...].astype(jnp.float32)).astype(jnp.bfloat16)
 
         @pl.when(s < steps - window)
         def _():

time: 108 us -> 107 us (level)
  no operation moved by 1% of the time
where the time goes in v7:
time: 107 us
  Pallas kernels  103 us (96%)
  local copies, waits for them, and re-layouts  3.15 us (3%)
    pallas_call x1, Pallas kernels, routed(): pl.pallas_call(functools.partial(kernel, experts), out_shape=(jax.ShapeDt...  103 us
    unnamed x4, local copies, waits for them, and re-layouts  3.15 us

profile of v7, /device:TPU:32, one launch (start us, length us, event | category | flops | bytes accessed | tf_op | source)
XLA Modules:
  0.0 107.0 jit_solution(2407879964902852406)
XLA Ops:
  0.6 103.2 %shard_map.95 = (f32[2,1,256]{2,1,0:T(1,128)}, bf16[1,160,1792]{2,1,0:T(8,128)(2,1)}) custom-call(bf16[2,32,7168]{2,1,0:T(8,128)(2,1)} %tokens.1, bf16[2,32,7168]{2,1,0:T(8,128)(2,1)} %cotangent.1, s32[2,2,32]{2,1,0:T(2,128)} %bitcast.2, bf16[2,2,32]{2,1,0:T(2,128)(2,1)} %bitcast.3, s32[1,3]{1,0:T(1,128)} %dropped_in.1, bf16[1,1792,256]{2,1,0:T(8,128)(2,1)} %gate_w.1, ...), custom_call_target="tpu_custom_call" | custom-call | flops 4000000000 | bytes 200000000 | tf_op jit(solution)/shard_map/pallas_call | solution.py:600
  103.8 0.0 copy-start
  103.8 0.7 copy-done
  104.5 0.6 copy.12
  105.0 1.9 %copy.13 = bf16[1,160,1792]{2,1,0:T(8,128)(2,1)} copy(bf16[1,160,1792]{2,1,0:T(8,128)(2,1)} %get-tuple-element.5) | data formatting | bytes 1146880
Async XLA Ops:
  103.8 0.7 copy-start
